TPU v7x, 512 devices: a whole 4x4x16 slice. The times are simulated.
512 devices in a mesh: gx: 32 (over x, y, core), gy: 16 (over z).
Axes of the slice: x: 4, y: 4, z: 16, core: 2. Of those that a mesh axis runs over, the one named last changes fastest.
Arguments:
- momenta: float32 [3, 16, 128, 4096], P(None, None, 'gy', 'gx'), may hold values from -6 to 6
- theta: float32 [16, 128, 4096], P(None, 'gy', 'gx'), may hold values from -6 to 6
- courant: float32 [3, 16, 128, 4096], P(None, None, 'gy', 'gx'), may hold values from -0.3 to 0.3
- density: float32 [16, 128, 4096], P(None, 'gy', 'gx'), may hold values from 0.8 to 1.6
- metric_diag: float32 [3, 16, 128, 4096], P(None, None, 'gy', 'gx'), may hold values from 0.5 to 2
- metric_cross: float32 [3, 16, 128, 4096], P(None, None, 'gy', 'gx'), may hold values from -0.2 to 0.2
Outputs:
- momenta_out: float32 [3, 16, 128, 4096], P(None, None, 'gy', 'gx')
- theta_out: float32 [16, 128, 4096], P(None, 'gy', 'gx')
- pressure: float32 [16, 128, 4096], P(None, 'gy', 'gx')
All inputs are finite; a program needn't handle non-finite values.
Results may differ from a plain program's by a relative error of at most 0.0003.
Values sent between devices are 32-bit elements; how exact they have to be, the bound alone decides.
No kernel may reach another device: no remote copies, remote signals or barrier semaphores. Data moves between devices by JAX's collectives and lax.ppermute only.
A program may use at most 64 MiB of HBM per device.

v0:
```python
import jax
import jax.numpy as jnp
from jax import lax
from jax.sharding import PartitionSpec as P

ITERS = 3


helm = 0.02


def extended(cells, sides, width):
    for axis, dim in sides:
        count = lax.axis_size(axis)
        head = lax.slice_in_dim(cells, 0, width, axis=dim)
        tail = lax.slice_in_dim(cells, cells.shape[dim] - width, cells.shape[dim], axis=dim)
        cells = jnp.concatenate(
            [
                lax.ppermute(tail, axis, [(i, (i + 1) % count) for i in range(count)]),
                cells,
                lax.ppermute(head, axis, [((i + 1) % count, i) for i in range(count)]),
            ],
            axis=dim,
        )
    return cells


def zshift(a, dz):
    if dz == 0:
        return a
    if dz > 0:
        return jnp.concatenate((a[..., dz:, :, :], jnp.zeros_like(a[..., :dz, :, :])), axis=-3)
    return jnp.concatenate((jnp.zeros_like(a[..., dz:, :, :]), a[..., :dz, :, :]), axis=-3)


def make_look(width, margin):

    def look(a, dz, dy, dx):
        span_y = a.shape[-2] - 2 * (width - margin)
        span_x = a.shape[-1] - 2 * (width - margin)
        start_y = width - margin + dy
        start_x = width - margin + dx
        return zshift(a[..., start_y : start_y + span_y, start_x : start_x + span_x], dz)

    return look


def donor(left, right, courant):
    return jnp.maximum(courant, 0.0) * left + jnp.minimum(courant, 0.0) * right


def antidiff(left, right, courant, dens_left, dens_right):
    return (
        0.5
        * (jnp.abs(courant) - courant * courant / (0.5 * (dens_left + dens_right)))
        * (right - left)
    )


def upwind_pass(look, field, dens, cx, cy, cz):
    centre = look(field, 0, 0, 0)
    fxr = donor(centre, look(field, 0, 0, 1), look(cx, 0, 0, 1))
    fxl = donor(look(field, 0, 0, -1), centre, look(cx, 0, 0, 0))
    fyr = donor(centre, look(field, 0, 1, 0), look(cy, 0, 1, 0))
    fyl = donor(look(field, 0, -1, 0), centre, look(cy, 0, 0, 0))
    fzr = donor(centre, look(field, 1, 0, 0), look(cz, 1, 0, 0))
    fzl = donor(look(field, -1, 0, 0), centre, look(cz, 0, 0, 0))
    return centre - (fxr - fxl + fyr - fyl + fzr - fzl) / look(dens, 0, 0, 0)


def anti_pass(look_new, look_old, first, dens, cx, cy, cz):
    centre = look_new(first, 0, 0, 0)
    here = look_old(dens, 0, 0, 0)
    axr = antidiff(
        centre, look_new(first, 0, 0, 1), look_old(cx, 0, 0, 1), here, look_old(dens, 0, 0, 1)
    )
    axl = antidiff(
        look_new(first, 0, 0, -1), centre, look_old(cx, 0, 0, 0), look_old(dens, 0, 0, -1), here
    )
    ayr = antidiff(
        centre, look_new(first, 0, 1, 0), look_old(cy, 0, 1, 0), here, look_old(dens, 0, 1, 0)
    )
    ayl = antidiff(
        look_new(first, 0, -1, 0), centre, look_old(cy, 0, 0, 0), look_old(dens, 0, -1, 0), here
    )
    azr = antidiff(
        centre, look_new(first, 1, 0, 0), look_old(cz, 1, 0, 0), here, look_old(dens, 1, 0, 0)
    )
    azl = antidiff(
        look_new(first, -1, 0, 0), centre, look_old(cz, 0, 0, 0), look_old(dens, -1, 0, 0), here
    )
    return centre - (axr - axl + ayr - ayl + azr - azl) / here


def coefficients(look, a_one, a_two, a_three, cross, upper_y, lower_y, upper_z, lower_z):
    wx = 0.5 * (look(a_one, 0, 0, 0) + look(a_one, 0, 0, 1))
    wxl = 0.5 * (look(a_one, 0, 0, -1) + look(a_one, 0, 0, 0))
    wy = 0.5 * (look(a_two, 0, 0, 0) + look(a_two, 0, 1, 0)) * upper_y
    wyl = 0.5 * (look(a_two, 0, -1, 0) + look(a_two, 0, 0, 0)) * lower_y
    wz = 0.5 * (a_three + zshift(a_three, 1)) * upper_z
    wzl = 0.5 * (zshift(a_three, -1) + a_three) * lower_z
    return (wx, wxl, wy, wyl, wz, wzl, cross[0], cross[1], cross[2])


def operate(look, field, coef):
    wx, wxl, wy, wyl, wz, wzl, c_xy, c_xz, c_yz = coef
    centre = look(field, 0, 0, 0)
    flow_x = wx * (look(field, 0, 0, 1) - centre) - wxl * (centre - look(field, 0, 0, -1))
    flow_y = wy * (look(field, 0, 1, 0) - centre) - wyl * (centre - look(field, 0, -1, 0))
    flow_z = wz * (look(field, 1, 0, 0) - centre) - wzl * (centre - look(field, -1, 0, 0))
    d_xy = 0.25 * (
        look(field, 0, 1, 1)
        - look(field, 0, 1, -1)
        - (look(field, 0, -1, 1) - look(field, 0, -1, -1))
    )
    d_xz = 0.25 * (
        look(field, 1, 0, 1)
        - look(field, 1, 0, -1)
        - (look(field, -1, 0, 1) - look(field, -1, 0, -1))
    )
    d_yz = 0.25 * (
        look(field, 1, 1, 0)
        - look(field, 1, -1, 0)
        - (look(field, -1, 1, 0) - look(field, -1, -1, 0))
    )
    return flow_x + flow_y + flow_z + c_xy * d_xy + c_xz * d_xz + c_yz * d_yz - helm * centre


def local(momenta, theta, courant, density, metric_diag, metric_cross):
    levels_count = density.shape[0]
    rows_dev = density.shape[1]
    total_rows = rows_dev * lax.axis_size("gy")
    first_row = lax.axis_index("gy") * rows_dev
    levels = jnp.arange(levels_count, dtype=jnp.int32)[:, None, None]
    level_mask = (levels != 0).astype(jnp.float32)
    packed = jnp.concatenate((momenta, theta[None], density[None], courant), axis=0)
    global_rows = first_row + jnp.arange(rows_dev + 2 * 1, dtype=jnp.int32) - 1
    inside = ((global_rows >= 0) & (global_rows < total_rows))[:, None]
    not_first = (global_rows != 0).astype(jnp.float32)[:, None]
    look_one = make_look(1, 0)
    narrow = extended(packed, (("gx", 3), ("gy", 2)), 1)
    narrow = jnp.where(inside, narrow, 0.0)
    dens_pad = narrow[4]
    cy_pad = narrow[6] * not_first
    cz_pad = narrow[7] * level_mask
    first = upwind_pass(look_one, narrow[0:4], dens_pad, narrow[5], cy_pad, cz_pad)
    first_pad = extended(first, (("gx", 3), ("gy", 2)), 1)
    first_pad = jnp.where(inside, first_pad, 0.0)
    moved = anti_pass(look_one, look_one, first_pad, dens_pad, narrow[5], cy_pad, cz_pad)
    flows = jnp.concatenate((moved[0:2], metric_diag[0:2]), axis=0)
    flows_pad = extended(flows, (("gx", 3), ("gy", 2)), 1)
    flows_pad = jnp.where(inside, flows_pad, 0.0)
    rhs = (
        0.5 * (look_one(flows_pad[0], 0, 0, 1) - look_one(flows_pad[0], 0, 0, -1))
        + 0.5 * (look_one(flows_pad[1], 0, 1, 0) - look_one(flows_pad[1], 0, -1, 0))
        + 0.5 * (zshift(moved[2], 1) - zshift(moved[2], -1))
    )
    global_rows = (first_row + jnp.arange(rows_dev, dtype=jnp.int32))[:, None]
    upper_y = (global_rows < total_rows - 1).astype(jnp.float32)
    lower_y = (global_rows > 0).astype(jnp.float32)
    upper_z = (levels < levels_count - 1).astype(jnp.float32)
    lower_z = (levels > 0).astype(jnp.float32)
    coef = coefficients(
        look_one,
        flows_pad[2],
        flows_pad[3],
        metric_diag[2],
        metric_cross,
        upper_y,
        lower_y,
        upper_z,
        lower_z,
    )

    def apply_operator(field):
        padded = extended(field, (("gx", 2), ("gy", 1)), 1)
        padded = jnp.where(inside, padded, 0.0)
        return (operate(look_one, padded, coef), padded)

    solution = jnp.zeros_like(rhs)
    resid = rhs
    dirs = [resid]
    first_image, first_pad_dir = apply_operator(resid)
    images = [first_image]
    along, norm_first = lax.psum(
        (jnp.sum(resid * images[0]), jnp.sum(images[0] * images[0])), ("gx", "gy")
    )
    norms = [norm_first]
    for step in range(ITERS):
        beta = along / norms[step]
        solution = solution + beta * dirs[step]
        resid = resid - beta * images[step]
        if step + 1 < ITERS:
            lifted, resid_pad = apply_operator(resid)
            alphas = []
            locals_proj = jnp.stack([jnp.sum(lifted * image) for image in images])
            totals = lax.psum(locals_proj, ("gx", "gy"))
            new_dir = resid
            new_img = lifted
            for back in range(step + 1):
                alpha = totals[back] / norms[back]
                alphas.append(alpha)
                new_dir = new_dir - alpha * dirs[back]
                new_img = new_img - alpha * images[back]
            along, new_norm = lax.psum(
                (jnp.sum(resid * new_img), jnp.sum(new_img * new_img)), ("gx", "gy")
            )
            dirs.append(new_dir)
            images.append(new_img)
            norms.append(new_norm)
    pressure_pad = extended(solution, (("gx", 2), ("gy", 1)), 1)
    pressure_pad = jnp.where(inside, pressure_pad, 0.0)
    grad_x = 0.5 * (look_one(pressure_pad, 0, 0, 1) - look_one(pressure_pad, 0, 0, -1))
    grad_y = 0.5 * (look_one(pressure_pad, 0, 1, 0) - look_one(pressure_pad, 0, -1, 0))
    grad_z = 0.5 * (zshift(solution, 1) - zshift(solution, -1))
    momenta_out = jnp.stack((moved[0] - grad_x, moved[1] - grad_y, moved[2] - grad_z), axis=0)
    return (momenta_out, moved[3], solution)


def solution(mesh):
    placed = (
        P(None, None, "gy", "gx"),
        P(None, "gy", "gx"),
        P(None, None, "gy", "gx"),
        P(None, "gy", "gx"),
        P(None, None, "gy", "gx"),
        P(None, None, "gy", "gx"),
    )
    return jax.shard_map(
        local,
        mesh=mesh,
        in_specs=placed,
        out_specs=(P(None, None, "gy", "gx"), P(None, "gy", "gx"), P(None, "gy", "gx")),
        check_vma=False,
    )
```

profile of v0, /device:TPU:1, one launch (start us, length us, event | category | flops | bytes accessed | tf_op | source)
XLA Modules:
  0.0 685.7 jit_solution(6977475944559347426)
XLA Ops:
  2.1 4.6 collective-permute-start
  6.7 6.1 collective-permute-start.1
  12.8 4.6 collective-permute-done.1
  18.4 3.3 collective-permute-start.2
  21.6 9.5 %collective-permute-start.3 = (f32[8,16,1,130]{3,2,1,0:T(1,128)S(1)}, f32[8,16,1,130]{3,2,1,0:T(1,128)S(1)}, u32[]{:S(2)}, u32[]{:S(2)}) collective-permute-start(f32[8,16,1,130]{3,2,1,0:T(1,128)S(1)} %get-tuple-element.33), channel_id=1, source_target_pairs={{1,0},{2,1},{3,2},{4,3},{5,4},{6,5},{7,6},{8,7},{9,8},{10,9},{11,1... | collective-permute-start | bytes 199688 | tf_op jit(solution)/shard_map/ppermute | solution.py:21
  35.6 3.1 collective-permute-start.4
  38.7 3.6 collective-permute-start.5
  42.3 4.4 collective-permute-done.5
  49.1 5.3 collective-permute-start.7
  59.3 6.9 collective-permute-start.9
  69.7 5.2 collective-permute-start.11
  79.4 10.2 %collective-permute-start.13 = (f32[16,8,1]{2,1,0:T(8,128)S(1)}, f32[16,8,1]{2,1,0:T(8,128)S(1)}, u32[]{:S(2)}, u32[]{:S(2)}) collective-permute-start(f32[16,8,1]{2,1,0:T(8,128)S(1)} %get-tuple-element.123), channel_id=1, source_target_pairs={{16,0},{32,16},{48,32},{64,48},{80,64},{96,80},{112,96},{128,112},... | collective-permute-start | bytes 1544 | tf_op jit(solution)/shard_map/ppermute | solution.py:21
  92.7 5.0 collective-permute-start.15
  99.9 110.8 %all-reduce.45 = (f32[]{:T(128)}, f32[]{:T(128)}) all-reduce(f32[]{:T(128)} %get-tuple-element.10, f32[]{:T(128)} %get-tuple-element.9), channel_id=1, replica_groups=mesh['gx'=32,'gy'=16] {'gx','gy'}, use_global_device_ids=true, to_apply=%region_1.2 | all-reduce | flops 2 | bytes 16 | tf_op jit(solution)/shard_map/psum | solution.py:185
  214.1 2.9 collective-permute-start.17
  221.7 4.6 collective-permute-start.19
  228.4 108.0 %psum.58 = f32[]{:T(128)} all-reduce(f32[]{:T(128)} %get-tuple-element.19), channel_id=1, replica_groups=mesh['gx'=32,'gy'=16] {'gx','gy'}, use_global_device_ids=true, to_apply=%region_5.6 | all-reduce | flops 1 | bytes 8 | tf_op jit(solution)/shard_map/psum | solution.py:197
  338.4 98.7 %all-reduce.44 = (f32[]{:T(128)}, f32[]{:T(128)}) all-reduce(f32[]{:T(128)} %get-tuple-element.8, f32[]{:T(128)} %get-tuple-element.7), channel_id=1, replica_groups=mesh['gx'=32,'gy'=16] {'gx','gy'}, use_global_device_ids=true, to_apply=%region_7.8 | all-reduce | flops 2 | bytes 16 | tf_op jit(solution)/shard_map/psum | solution.py:205
  443.3 3.9 collective-permute-done.21
  447.4 3.7 collective-permute-start.22
  458.3 105.6 %psum.61 = f32[2]{0:T(128)S(1)} all-reduce(f32[2]{0:T(128)S(1)} %pad_maximum_fusion.29), channel_id=1, replica_groups=mesh['gx'=32,'gy'=16] {'gx','gy'}, use_global_device_ids=true, to_apply=%region_12.13 | all-reduce | flops 2 | bytes 16 | tf_op jit(solution)/shard_map/psum | solution.py:197
  567.8 98.8 %all-reduce.43 = (f32[]{:T(128)}, f32[]{:T(128)}) all-reduce(f32[]{:T(128)} %get-tuple-element.4, f32[]{:T(128)} %get-tuple-element.3), channel_id=1, replica_groups=mesh['gx'=32,'gy'=16] {'gx','gy'}, use_global_device_ids=true, to_apply=%region_14.15 | all-reduce | flops 2 | bytes 16 | tf_op jit(solution)/shard_map/psum | solution.py:205
  673.2 3.2 collective-permute-done.25
  676.6 3.7 collective-permute-start.26
  (111 shorter events, 60.9 us)
Async XLA Ops:
  2.1 10.7 %collective-permute-start = (f32[8,16,8,1]{3,2,1,0:T(8,128)S(1)}, f32[8,16,8,1]{3,2,1,0:T(8,128)S(1)}, u32[]{:S(2)}, u32[]{:S(2)}) collective-permute-start(f32[8,16,8,1]{3,2,1,0:T(8,128)S(1)} %get-tuple-element.50), channel_id=1, source_target_pairs={{0,16},{16,32},{32,48},{48,64},{64,80},{80,96},{96,112},{112,128},... | collective-permute-start | bytes 12296 | tf_op jit(solution)/shard_map/ppermute | solution.py:19
  6.7 10.8 %collective-permute-start.1 = (f32[8,16,8,1]{3,2,1,0:T(8,128)S(1)}, f32[8,16,8,1]{3,2,1,0:T(8,128)S(1)}, u32[]{:S(2)}, u32[]{:S(2)}) collective-permute-start(f32[8,16,8,1]{3,2,1,0:T(8,128)S(1)} %get-tuple-element.51), channel_id=1, source_target_pairs={{16,0},{32,16},{48,32},{64,48},{80,64},{96,80},{112,96},{128,112},... | collective-permute-start | bytes 12296 | tf_op jit(solution)/shard_map/ppermute | solution.py:21
  18.4 13.2 %collective-permute-start.2 = (f32[8,16,1,130]{3,2,1,0:T(1,128)S(1)}, f32[8,16,1,130]{3,2,1,0:T(1,128)S(1)}, u32[]{:S(2)}, u32[]{:S(2)}) collective-permute-start(f32[8,16,1,130]{3,2,1,0:T(1,128)S(1)} %get-tuple-element.32), channel_id=1, source_target_pairs={{0,1},{1,2},{2,3},{3,4},{4,5},{5,6},{6,7},{7,8},{8,9},{9,10},{10,1... | collective-permute-start | bytes 199688 | tf_op jit(solution)/shard_map/ppermute | solution.py:19
  21.6 11.4 %collective-permute-start.3 = (f32[8,16,1,130]{3,2,1,0:T(1,128)S(1)}, f32[8,16,1,130]{3,2,1,0:T(1,128)S(1)}, u32[]{:S(2)}, u32[]{:S(2)}) collective-permute-start(f32[8,16,1,130]{3,2,1,0:T(1,128)S(1)} %get-tuple-element.33), channel_id=1, source_target_pairs={{1,0},{2,1},{3,2},{4,3},{5,4},{6,5},{7,6},{8,7},{9,8},{10,9},{11,1... | collective-permute-start | bytes 199688 | tf_op jit(solution)/shard_map/ppermute | solution.py:21
  35.6 6.7 collective-permute-start.4
  38.7 8.0 %collective-permute-start.5 = (f32[4,16,8,1]{3,2,1,0:T(8,128)S(1)}, f32[4,16,8,1]{3,2,1,0:T(8,128)S(1)}, u32[]{:S(2)}, u32[]{:S(2)}) collective-permute-start(f32[4,16,8,1]{3,2,1,0:T(8,128)S(1)} %get-tuple-element.103), channel_id=1, source_target_pairs={{16,0},{32,16},{48,32},{64,48},{80,64},{96,80},{112,96},{128,112},... | collective-permute-start | bytes 6152 | tf_op jit(solution)/shard_map/ppermute | solution.py:21
  47.1 7.3 %collective-permute-start.6 = (f32[4,16,1,130]{3,2,1,0:T(1,128)S(1)}, f32[4,16,1,130]{3,2,1,0:T(1,128)S(1)}, u32[]{:S(2)}, u32[]{:S(2)}) collective-permute-start(f32[4,16,1,130]{3,2,1,0:T(1,128)S(1)} %get-tuple-element.42), channel_id=1, source_target_pairs={{0,1},{1,2},{2,3},{3,4},{4,5},{5,6},{6,7},{7,8},{8,9},{9,10},{10,1... | collective-permute-start | bytes 99848 | tf_op jit(solution)/shard_map/ppermute | solution.py:19
  49.1 6.6 collective-permute-start.7
  57.0 9.2 %collective-permute-start.8 = (f32[4,16,8,1]{3,2,1,0:T(8,128)S(1)}, f32[4,16,8,1]{3,2,1,0:T(8,128)S(1)}, u32[]{:S(2)}, u32[]{:S(2)}) collective-permute-start(f32[4,16,8,1]{3,2,1,0:T(8,128)S(1)} %get-tuple-element.83), channel_id=1, source_target_pairs={{0,16},{16,32},{32,48},{48,64},{64,80},{80,96},{96,112},{112,128},... | collective-permute-start | bytes 6152 | tf_op jit(solution)/shard_map/ppermute | solution.py:19
  59.3 8.0 %collective-permute-start.9 = (f32[4,16,8,1]{3,2,1,0:T(8,128)S(1)}, f32[4,16,8,1]{3,2,1,0:T(8,128)S(1)}, u32[]{:S(2)}, u32[]{:S(2)}) collective-permute-start(f32[4,16,8,1]{3,2,1,0:T(8,128)S(1)} %get-tuple-element.84), channel_id=1, source_target_pairs={{16,0},{32,16},{48,32},{64,48},{80,64},{96,80},{112,96},{128,112},... | collective-permute-start | bytes 6152 | tf_op jit(solution)/shard_map/ppermute | solution.py:21
  67.8 7.2 %collective-permute-start.10 = (f32[4,16,1,130]{3,2,1,0:T(1,128)S(1)}, f32[4,16,1,130]{3,2,1,0:T(1,128)S(1)}, u32[]{:S(2)}, u32[]{:S(2)}) collective-permute-start(f32[4,16,1,130]{3,2,1,0:T(1,128)S(1)} %get-tuple-element.40), channel_id=1, source_target_pairs={{0,1},{1,2},{2,3},{3,4},{4,5},{5,6},{6,7},{7,8},{8,9},{9,10},{10,1... | collective-permute-start | bytes 99848 | tf_op jit(solution)/shard_map/ppermute | solution.py:19
  69.7 6.5 collective-permute-start.11
  77.1 12.5 %collective-permute-start.12 = (f32[16,8,1]{2,1,0:T(8,128)S(1)}, f32[16,8,1]{2,1,0:T(8,128)S(1)}, u32[]{:S(2)}, u32[]{:S(2)}) collective-permute-start(f32[16,8,1]{2,1,0:T(8,128)S(1)} %get-tuple-element.122), channel_id=1, source_target_pairs={{0,16},{16,32},{32,48},{48,64},{64,80},{80,96},{96,112},{112,128},... | collective-permute-start | bytes 1544 | tf_op jit(solution)/shard_map/ppermute | solution.py:19
  79.4 11.1 %collective-permute-start.13 = (f32[16,8,1]{2,1,0:T(8,128)S(1)}, f32[16,8,1]{2,1,0:T(8,128)S(1)}, u32[]{:S(2)}, u32[]{:S(2)}) collective-permute-start(f32[16,8,1]{2,1,0:T(8,128)S(1)} %get-tuple-element.123), channel_id=1, source_target_pairs={{16,0},{32,16},{48,32},{64,48},{80,64},{96,80},{112,96},{128,112},... | collective-permute-start | bytes 1544 | tf_op jit(solution)/shard_map/ppermute | solution.py:21
  90.6 7.2 %collective-permute-start.14 = (f32[16,1,130]{2,1,0:T(1,128)S(1)}, f32[16,1,130]{2,1,0:T(1,128)S(1)}, u32[]{:S(2)}, u32[]{:S(2)}) collective-permute-start(f32[16,1,130]{2,1,0:T(1,128)S(1)} %get-tuple-element.112), channel_id=1, source_target_pairs={{0,1},{1,2},{2,3},{3,4},{4,5},{5,6},{6,7},{7,8},{8,9},{9,10},{10,1... | collective-permute-start | bytes 24968 | tf_op jit(solution)/shard_map/ppermute | solution.py:19
  92.7 5.8 collective-permute-start.15
  214.1 5.6 collective-permute-start.17
  219.8 6.5 collective-permute-start.18
  221.7 5.4 collective-permute-start.19
  441.4 5.9 collective-permute-start.21
  447.4 6.5 collective-permute-start.22
  668.1 5.2 collective-permute-start.24
  670.5 5.9 collective-permute-start.25
  676.6 6.5 collective-permute-start.26
  (11 other events, 145.2 us)
where the time goes:
time: 690 us; the launch traced here: 686 us
  blocking collectives  522 us (76%)
  starting transfers between devices  107 us (16%)
  waiting for transfers between devices  30.2 us (4%)
  other arithmetic  14.3 us (2%)
  between operations  9.39 us (1%)
    psum x2, blocking collectives, local(): totals = lax.psum(locals_proj, ('gx', 'gy'))  214 us
    psum x2, blocking collectives, local(): lax.psum((jnp.sum(resid * new_img), jnp.sum(new_img * new_img)), ('gx', '...  197 us
    psum x1, blocking collectives, local(): lax.psum((jnp.sum(resid * images[0]), jnp.sum(images[0] * images[0])), ('...  111 us
    ppermute x14, starting transfers between devices, extended(): lax.ppermute(head, axis, [((i + 1) % count, i) for i in range(count)])  68.8 us
    ppermute x14, starting transfers between devices, extended(): lax.ppermute(tail, axis, [(i, (i + 1) % count) for i in range(count)])  38 us
    ppermute x14, waiting for transfers between devices, extended(): lax.ppermute(head, axis, [((i + 1) % count, i) for i in range(count)])  29.7 us
  transfers between devices with their start and end apart: 28, of which 15 were waited for; matrix products, arithmetic and copies ran while one was open for 0% of the time, Pallas kernels for 0%

commit v1 on v0

v1 whole, which is shorter than its diff:
```python
import jax
import jax.numpy as jnp
from jax import lax
from jax.experimental import pallas as pl
from jax.experimental.pallas import tpu as pltpu
from jax.sharding import PartitionSpec as P

helm = 0.02
ITERS = 3
NF = 14
U, V, W, TH, G, CX, CY, CZ, A11, A22, A33, A12, A13, A23 = range(NF)
COMBOS = (
    (V, 6, TH, 2),
    (CY, 6, A12, 2),
    (U, 5, A22, 3),
    (W, 5, A11, 2),
    (G, 5, A33, 2),
    (CX, 5, A13, 2),
    (CZ, 5, A23, 2),
)
F32 = jnp.float32


def lanes(shape):
    return lax.broadcasted_iota(jnp.int32, shape, len(shape) - 1)


def rows(shape):
    return lax.broadcasted_iota(jnp.int32, shape, len(shape) - 2)


def roll(a, shift, axis):
    shift = shift % a.shape[axis]
    if shift == 0:
        return a
    return pltpu.roll(a, shift, axis)


def xs(a, d):
    return roll(a, -d, 1)


def ys(a, d):
    return roll(a, -d, 0)


def field_of(refs, f):
    mom, th, cou, den, dia, cro = refs
    if f < 3:
        return mom.at[f]
    if f == TH:
        return th
    if f == G:
        return den
    if f < 8:
        return cou.at[f - 5]
    if f < 11:
        return dia.at[f - 8]
    return cro.at[f - 11]


def pack_kernel(mom, th, cou, den, dia, cro, to_left, to_right, to_up, to_down):
    refs = (mom, th, cou, den, dia, cro)
    nz = den.shape[0]
    lane = lanes((8, 128)) // 8
    row = rows((8, 128))
    for f in range(NF):
        ref = field_of(refs, f)
        left = jnp.zeros((8, 128), F32)
        right = jnp.zeros((8, 128), F32)
        for k in range(nz):
            moved = roll(ref[k], 8 * k, 1)
            left = jnp.where(lane == k, moved, left)
            right = jnp.where(lane == (k - 1) % nz, moved, right)
        to_left[f] = left
        to_right[f] = right
    for c, (first, n, second, m) in enumerate(COMBOS):
        one, two = field_of(refs, first), field_of(refs, second)
        for k in range(nz):
            a, b = one[k], two[k]
            to_down[c, k] = jnp.where(row < n, a, roll(b, n, 0))
            to_up[c, k] = jnp.where(row >= 8 - n, a, roll(b, -n, 0))


def main_kernel(
    mom, th, cou, den, dia, cro, from_left, from_right, below, above, cbelow, cabove,
    moved, theta_out, basis, dxs, dys, gram,
    S, P1, M, IG, C, VV, D, E, T,
):
    refs = (mom, th, cou, den, dia, cro)
    nz = den.shape[0]
    gy = lax.axis_index("gy")
    ny = lax.axis_size("gy")
    has_below = gy > 0
    has_above = gy < ny - 1
    shape = (24, 256)
    lane128 = lanes((8, 128))
    row24 = rows(shape)
    inside = ((row24 >= 8) | has_below) & ((row24 < 16) | has_above)
    edge_row = ((row24 == 8) & ~has_below) | ((row24 == 16) & ~has_above)

    for c, (first, n, second, m) in enumerate(COMBOS):
        for f, shift in ((first, 0), (second, n)):
            ref = field_of(refs, f)
            outside = 1.0 if f == G else 0.0

            def rows_in(k, carry, f=f, shift=shift, c=c, ref=ref, outside=outside):
                low = roll(below[c, k], shift, 0)
                high = roll(above[c, k], -shift, 0)
                S[f, k + 1, 0:8, 0:128] = jnp.where(has_below, low, outside)
                S[f, k + 1, 8:16, 0:128] = ref[k]
                S[f, k + 1, 16:24, 0:128] = jnp.where(has_above, high, outside)
                return carry

            lax.fori_loop(0, nz, rows_in, 0, unroll=True)
    for f in range(NF):
        outside = 1.0 if f == G else 0.0
        for g, (left, right) in enumerate(
            (
                (cbelow[f], cbelow[NF + f]),
                (from_left[f], from_right[f]),
                (cabove[f], cabove[NF + f]),
            )
        ):
            if g == 0:
                left, right = (jnp.where(has_below, a, outside) for a in (left, right))
            if g == 2:
                left, right = (jnp.where(has_above, a, outside) for a in (left, right))
            for k in range(nz):
                S[f, k + 1, 8 * g : 8 * g + 8, 128:256] = jnp.where(
                    lane128 < 64, roll(right, -8 * k, 1), roll(left, -8 * k, 1)
                )
        pad = jnp.full(shape, outside, F32)
        S[f, 0] = pad
        S[f, nz + 1] = pad
    zero = jnp.zeros(shape, F32)
    S[CZ, 1] = zero

    def upwind(k, fz):
        cx, cy, cz = S[CX, k], S[CY, k], S[CZ, k + 1]
        cy = jnp.where(edge_row, 0.0, cy)
        S[CY, k] = cy
        ig = 1.0 / S[G, k]
        IG[k] = ig
        xp, xm = jnp.maximum(cx, 0.0), jnp.minimum(cx, 0.0)
        yp, ym = jnp.maximum(cy, 0.0), jnp.minimum(cy, 0.0)
        zp, zm = jnp.maximum(cz, 0.0), jnp.minimum(cz, 0.0)
        out = []
        for f in range(4):
            psi = S[f, k]
            fx = xp * xs(psi, -1) + xm * psi
            fy = yp * ys(psi, -1) + ym * psi
            up = zp * psi + zm * S[f, k + 1]
            P1[f, k] = psi - (xs(fx, 1) - fx + ys(fy, 1) - fy + up - fz[f]) * ig
            out.append(up)
        return tuple(out)

    lax.fori_loop(1, nz + 1, upwind, (zero,) * 4)
    for f in range(4):
        P1[f, 0] = zero
        P1[f, nz + 1] = zero

    def face(c, one, two):
        return 0.5 * (jnp.abs(c) - c * c / (0.5 * (one + two)))

    def anti(k, az):
        dens = S[G, k]
        kx = face(S[CX, k], xs(dens, -1), dens)
        ky = face(S[CY, k], ys(dens, -1), dens)
        kz = face(S[CZ, k + 1], dens, S[G, k + 1])
        ig = IG[k]
        out = []
        for f in range(4):
            psi = P1[f, k]
            ax = kx * (psi - xs(psi, -1))
            ay = ky * (psi - ys(psi, -1))
            up = kz * (P1[f, k + 1] - psi)
            res = psi - (xs(ax, 1) - ax + ys(ay, 1) - ay + up - az[f]) * ig
            if f < 3:
                M[f, k] = res
                moved[f, k - 1] = res[8:16, 0:128]
            else:
                theta_out[k - 1] = res[8:16, 0:128]
            out.append(up)
        return tuple(out)

    lax.fori_loop(1, nz + 1, anti, (zero,) * 4)
    M[2, 0] = zero
    M[2, nz + 1] = zero

    def first(k, carry):
        u, v = M[0, k], M[1, k]
        rhs = 0.5 * (
            (xs(u, 1) - xs(u, -1)) + (ys(v, 1) - ys(v, -1)) + (M[2, k + 1] - M[2, k - 1])
        )
        VV[0, k] = jnp.where(inside, rhs, 0.0)
        a11, a22, a33 = S[A11, k], S[A22, k], S[A33, k]
        wxl = 0.5 * (xs(a11, -1) + a11)
        wyl = jnp.where(edge_row, 0.0, 0.5 * (ys(a22, -1) + a22))
        wzl = jnp.where(k > 1, 0.5 * (S[A33, k - 1] + a33), 0.0)
        wz = jnp.where(k < nz, 0.5 * (S[A33, k + 1] + a33), 0.0)
        wx, wy = xs(wxl, 1), ys(wyl, 1)
        C[0, k] = wx
        C[1, k] = wxl
        C[2, k] = wy
        C[3, k] = wyl
        C[4, k] = wz
        C[5, k] = wzl
        C[6, k] = ((wx + wxl) + (wy + wyl)) + ((wz + wzl) + helm)
        C[7, k] = 0.25 * S[A12, k]
        C[8, k] = 0.25 * S[A13, k]
        C[9, k] = 0.25 * S[A23, k]
        return carry

    lax.fori_loop(1, nz + 1, first, 0)
    for i in range(3):
        VV[i, 0] = zero
        VV[i, nz + 1] = zero
    for a in (D, E):
        a[0] = zero
        a[nz + 1] = zero

    own = lambda a: a[8:16, 0:128]
    sums = {}
    for i in range(3):
        last = i == 2
        cut = own if last else (lambda a: a)

        def flat(k, carry, i=i, cut=cut):
            p = VV[i, k]
            xp, xm, yp, ym = xs(p, 1), xs(p, -1), ys(p, 1), ys(p, -1)
            d, e = xp - xm, yp - ym
            D[k] = d
            E[k] = e
            dxs[i, k - 1] = own(d)
            dys[i, k - 1] = own(e)
            basis[i, k - 1] = own(p)
            dxy = ys(d, 1) - ys(d, -1)
            c = [cut(C[n, k]) for n in range(8)]
            t = (c[0] * cut(xp) + c[1] * cut(xm)) + (c[2] * cut(yp) + c[3] * cut(ym))
            t = t + (c[4] * cut(VV[i, k + 1]) + c[5] * cut(VV[i, k - 1]))
            t = t - c[6] * cut(p) + c[7] * cut(dxy)
            if t.shape == (8, 128):
                T[k, 8:16, 0:128] = t
            else:
                T[k] = t
            return carry

        lax.fori_loop(1, nz + 1, flat, 0)

        pairs = [(j, i + 1) for j in range(i + 2)]

        def deep(k, acc, i=i, cut=cut, last=last, pairs=pairs):
            v = cut(T[k]) + cut(C[8, k]) * (cut(D[k + 1]) - cut(D[k - 1]))
            v = v + cut(C[9, k]) * (cut(E[k + 1]) - cut(E[k - 1]))
            if not last:
                VV[i + 1, k] = v
                v = own(v)
            vs = [own(VV[j, k]) for j in range(i + 1)] + [v]
            return tuple(s + vs[j] * v for s, (j, _) in zip(acc, pairs))

        acc = lax.fori_loop(1, nz + 1, deep, (jnp.zeros((8, 128), F32),) * len(pairs))
        for s, key in zip(acc, pairs):
            sums[key] = s
    line = lanes((1, 128))
    out = jnp.zeros((1, 128), F32)
    for n, key in enumerate(KEYS):
        s = jnp.sum(jnp.sum(sums[key], axis=0, keepdims=True), axis=1, keepdims=True)
        out = jnp.where(line == n, s, out)
    gram[...] = jnp.broadcast_to(out, gram.shape)


KEYS = ((0, 1), (1, 1), (0, 2), (1, 2), (2, 2), (0, 3), (1, 3), (2, 3), (3, 3))


def weights(gram):
    def inner(a, b):
        total = 0.0
        for i in range(4):
            for j in range(4):
                if a[i] is not None and b[j] is not None:
                    total = total + a[i] * b[j] * gram[(min(i, j), max(i, j))]
        return total

    def less(a, s, b):
        out = []
        for one, two in zip(a, b):
            if two is None:
                out.append(one)
            else:
                out.append(-(s * two) if one is None else one - s * two)
        return out

    one = jnp.ones((1, 1), F32)
    r = [one, None, None, None]
    sol = [None] * 4
    dirs, images, norms = [r], [[None, one, None, None]], []
    for n in range(ITERS):
        norms.append(inner(images[n], images[n]))
        beta = inner(r, images[n]) / norms[n]
        sol = less(sol, -beta, dirs[n])
        r = less(r, beta, images[n])
        if n + 1 < ITERS:
            z = [None] + r[:3]
            new_dir, new_img = r, z
            for l in range(n + 1):
                alpha = inner(z, images[l]) / norms[l]
                new_dir = less(new_dir, alpha, dirs[l])
                new_img = less(new_img, alpha, images[l])
            dirs.append(new_dir)
            images.append(new_img)
    return sol[:3]


def last_kernel(partial, moved, basis, dxs, dys, momenta_out, pressure):
    nz = moved.shape[1]
    total = jnp.sum(partial[...], axis=0, keepdims=True)
    line = lanes(total.shape)
    gram = {
        key: jnp.sum(jnp.where(line == n, total, 0.0), axis=1, keepdims=True)
        for n, key in enumerate(KEYS)
    }
    c = [jnp.broadcast_to(s, (8, 128)) for s in weights(gram)]
    p = [(c[0] * basis[0, k] + c[1] * basis[1, k]) + c[2] * basis[2, k] for k in range(nz)]
    h = [0.5 * s for s in c]
    zero = jnp.zeros((8, 128), F32)
    for k in range(nz):
        pressure[k] = p[k]
        dx = (h[0] * dxs[0, k] + h[1] * dxs[1, k]) + h[2] * dxs[2, k]
        dy = (h[0] * dys[0, k] + h[1] * dys[1, k]) + h[2] * dys[2, k]
        above = p[k + 1] if k + 1 < nz else zero
        below = p[k - 1] if k > 0 else zero
        momenta_out[0, k] = moved[0, k] - dx
        momenta_out[1, k] = moved[1, k] - dy
        momenta_out[2, k] = moved[2, k] - 0.5 * (above - below)


def shift_to(a, axis, step):
    n = lax.axis_size(axis)
    return lax.ppermute(a, axis, [(i, (i + step) % n) for i in range(n)])


def local(momenta, theta, courant, density, metric_diag, metric_cross):
    nz = density.shape[0]
    vm = pl.BlockSpec(memory_space=pltpu.VMEM)
    args = (momenta, theta, courant, density, metric_diag, metric_cross)
    sds = jax.ShapeDtypeStruct
    nc = len(COMBOS)
    to_left, to_right, to_up, to_down = pl.pallas_call(
        pack_kernel,
        out_shape=(sds((NF, 8, 128), F32),) * 2 + (sds((nc, nz, 8, 128), F32),) * 2,
        in_specs=[vm] * 6,
        out_specs=[vm] * 4,
        compiler_params=pltpu.CompilerParams(vmem_limit_bytes=16 << 20),
        name="pack",
    )(*args)
    from_left = shift_to(to_right, "gx", 1)
    from_right = shift_to(to_left, "gx", -1)
    below = shift_to(to_up, "gy", 1)
    above = shift_to(to_down, "gy", -1)
    sides = jnp.concatenate((from_left, from_right), axis=0)
    cbelow = shift_to(sides, "gy", 1)
    cabove = shift_to(sides, "gy", -1)

    block = (nz, 8, 128)
    big = (nz + 2, 24, 256)
    nx, ny = lax.axis_size("gx"), lax.axis_size("gy")
    moved, theta_out, basis, dxs, dys, gram = pl.pallas_call(
        main_kernel,
        out_shape=(
            sds((3,) + block, F32),
            sds(block, F32),
            sds((3,) + block, F32),
            sds((3,) + block, F32),
            sds((3,) + block, F32),
            sds((nx, 128), F32),
        ),
        in_specs=[vm] * 12,
        out_specs=[vm] * 6,
        scratch_shapes=[
            pltpu.VMEM((NF,) + big, F32),
            pltpu.VMEM((4,) + big, F32),
            pltpu.VMEM((3,) + big, F32),
            pltpu.VMEM(big, F32),
            pltpu.VMEM((10,) + big, F32),
            pltpu.VMEM((3,) + big, F32),
            pltpu.VMEM(big, F32),
            pltpu.VMEM(big, F32),
            pltpu.VMEM(big, F32),
        ],
        compiler_params=pltpu.CompilerParams(vmem_limit_bytes=40 << 20),
        name="advance",
    )(*args, from_left, from_right, below, above, cbelow, cabove)

    part = lax.all_to_all(gram, "gx", 0, 0, tiled=True)
    part = jnp.broadcast_to(jnp.sum(part, axis=0, keepdims=True), (ny, 128))
    part = lax.all_to_all(part, "gy", 0, 0, tiled=True)

    momenta_out, pressure = pl.pallas_call(
        last_kernel,
        out_shape=(sds((3,) + block, F32), sds(block, F32)),
        in_specs=[vm] * 5,
        out_specs=[vm] * 2,
        compiler_params=pltpu.CompilerParams(vmem_limit_bytes=16 << 20),
        name="combine",
    )(part, moved, basis, dxs, dys)
    return (momenta_out, theta_out, pressure)


def solution(mesh):
    placed = (
        P(None, None, "gy", "gx"),
        P(None, "gy", "gx"),
        P(None, None, "gy", "gx"),
        P(None, "gy", "gx"),
        P(None, None, "gy", "gx"),
        P(None, None, "gy", "gx"),
    )
    return jax.shard_map(
        local,
        mesh=mesh,
        in_specs=placed,
        out_specs=(P(None, None, "gy", "gx"), P(None, "gy", "gx"), P(None, "gy", "gx")),
        check_vma=False,
    )
```

time: 690 us -> 90.7 us (0.13)
  blocking collectives: 522 us -> 33.1 us
  starting transfers between devices: 107 us -> 25.8 us
  waiting for transfers between devices: 30.2 us -> 8.36 us
  Pallas kernels: 0 us -> 16.6 us
  other arithmetic: 14.3 us -> 0.05 us
  between operations: 9.39 us -> 0.79 us
    psum x5 -> x0, blocking collectives: 522 us -> none  [the longest x2 214 us: local(): totals = lax.psum(locals_proj, ('gx', 'gy'))]
    ppermute x28 -> x6, starting transfers between devices: 107 us -> 25.8 us  [shift_to(): return lax.ppermute(a, axis, [(i, (i + step) % n) for i in range(n)])]
    all_to_all x0 -> x2, blocking collectives: none -> 33.1 us  [the longest x1 18 us: local(): part = lax.all_to_all(part, 'gy', 0, 0, tiled=True)]
    ppermute x28 -> x6, waiting for transfers between devices: 30.2 us -> 8.36 us  [shift_to(): return lax.ppermute(a, axis, [(i, (i + step) % n) for i in range(n)])]
    pallas_call x0 -> x3, Pallas kernels: none -> 16.6 us  [the longest x1 15.4 us: local(): pl.pallas_call(main_kernel, out_shape=(sds((3,) + block, F32), sds(block,...]
  transfers between devices with their start and end apart: 28 -> 6, of which waited for: 15 -> 2; matrix products, arithmetic and copies ran while one was open for 0% -> 0% of each run, Pallas kernels for 0% -> 0%
where the time goes in v1:
time: 90.7 us; the launch traced here: 90.1 us
  blocking collectives  33.1 us (36%)
  starting transfers between devices  25.8 us (28%)
  Pallas kernels  16.6 us (18%)
  waiting for transfers between devices  8.36 us (9%)
  local copies, waits for them, and re-layouts  5.42 us (6%)
    ppermute x6, starting transfers between devices, shift_to(): return lax.ppermute(a, axis, [(i, (i + step) % n) for i in range(n)])  25.8 us
    all_to_all x1, blocking collectives, local(): part = lax.all_to_all(part, 'gy', 0, 0, tiled=True)  18 us
    pallas_call x1, Pallas kernels, local(): pl.pallas_call(main_kernel, out_shape=(sds((3,) + block, F32), sds(block,...  15.4 us
    all_to_all x1, blocking collectives, local(): part = lax.all_to_all(gram, 'gx', 0, 0, tiled=True)  15.1 us
    ppermute x6, waiting for transfers between devices, shift_to(): return lax.ppermute(a, axis, [(i, (i + step) % n) for i in range(n)])  8.36 us
    unnamed x25, local copies, waits for them, and re-layouts  5.41 us
  transfers between devices with their start and end apart: 6, of which 2 were waited for; matrix products, arithmetic and copies ran while one was open for 0% of the time, Pallas kernels for 0%

profile of v1, /device:TPU:1, one launch (start us, length us, event | category | flops | bytes accessed | tf_op | source)
XLA Modules:
  0.0 90.1 jit_solution(7320428314247622506)
XLA Ops:
  0.6 0.0 copy-start
  0.6 0.9 %copy-done = f32[3,16,8,128]{3,2,1,0:T(8,128)S(1)} copy-done((f32[3,16,8,128]{3,2,1,0:T(8,128)S(1)}, f32[3,16,8,128]{3,2,1,0:T(8,128)}, u32[]{:S(2)}) %copy-start) | copy-done | bytes 196632
  1.6 0.9 %copy-done.2 = f32[3,16,8,128]{3,2,1,0:T(8,128)S(1)} copy-done((f32[3,16,8,128]{3,2,1,0:T(8,128)S(1)}, f32[3,16,8,128]{3,2,1,0:T(8,128)}, u32[]{:S(2)}) %copy-start.2) | copy-done | bytes 196632
  2.5 0.9 %copy-done.4 = f32[3,16,8,128]{3,2,1,0:T(8,128)S(1)} copy-done((f32[3,16,8,128]{3,2,1,0:T(8,128)S(1)}, f32[3,16,8,128]{3,2,1,0:T(8,128)}, u32[]{:S(2)}) %copy-start.4) | copy-done | bytes 196632
  3.4 0.9 %copy-done.6 = f32[3,16,8,128]{3,2,1,0:T(8,128)S(1)} copy-done((f32[3,16,8,128]{3,2,1,0:T(8,128)S(1)}, f32[3,16,8,128]{3,2,1,0:T(8,128)}, u32[]{:S(2)}) %copy-start.6) | copy-done | bytes 196632
  4.3 0.8 copy-done.8
  5.2 0.8 copy-done.10
  6.0 0.3 pack.1
  6.3 0.0 copy-start.1
  6.4 4.5 %collective-permute-start.2 = (f32[7,16,8,128]{3,2,1,0:T(8,128)S(1)}, f32[7,16,8,128]{3,2,1,0:T(8,128)S(1)}, u32[]{:S(2)}, u32[]{:S(2)}) collective-permute-start(f32[7,16,8,128]{3,2,1,0:T(8,128)S(1)} %get-tuple-element.17), channel_id=1, source_target_pairs={{0,1},{1,2},{2,3},{3,4},{4,5},{5,6},{6,7},{7,8},{8,9},{9,10},{10,1... | collective-permute-start | bytes 1376264 | tf_op jit(solution)/shard_map/ppermute | solution.py:340
  10.9 9.5 %collective-permute-start.3 = (f32[7,16,8,128]{3,2,1,0:T(8,128)S(1)}, f32[7,16,8,128]{3,2,1,0:T(8,128)S(1)}, u32[]{:S(2)}, u32[]{:S(2)}) collective-permute-start(f32[7,16,8,128]{3,2,1,0:T(8,128)S(1)} %get-tuple-element.18), channel_id=1, source_target_pairs={{0,15},{1,0},{2,1},{3,2},{4,3},{5,4},{6,5},{7,6},{8,7},{9,8},{10,9... | collective-permute-start | bytes 1376264 | tf_op jit(solution)/shard_map/ppermute | solution.py:340
  20.4 4.0 %collective-permute-start = (f32[14,8,128]{2,1,0:T(8,128)S(1)}, f32[14,8,128]{2,1,0:T(8,128)S(1)}, u32[]{:S(2)}, u32[]{:S(2)}) collective-permute-start(f32[14,8,128]{2,1,0:T(8,128)S(1)} %get-tuple-element.15), channel_id=1, source_target_pairs={{0,16},{16,32},{32,48},{48,64},{64,80},{80,96},{96,112},{112,128},... | collective-permute-start | bytes 172040 | tf_op jit(solution)/shard_map/ppermute | solution.py:340
  24.4 1.9 %collective-permute-start.1 = (f32[14,8,128]{2,1,0:T(8,128)S(1)}, f32[14,8,128]{2,1,0:T(8,128)S(1)}, u32[]{:S(2)}, u32[]{:S(2)}) collective-permute-start(f32[14,8,128]{2,1,0:T(8,128)S(1)} %get-tuple-element.16), channel_id=1, source_target_pairs={{0,496},{16,0},{32,16},{48,32},{64,48},{80,64},{96,80},{112,96},{1... | collective-permute-start | bytes 172040 | tf_op jit(solution)/shard_map/ppermute | solution.py:340
  26.4 0.0 collective-permute-done.from_left
  26.4 3.5 %collective-permute-done.1.from_right = f32[14,8,128]{2,1,0:T(8,128)S(1)} collective-permute-done((f32[14,8,128]{2,1,0:T(8,128)S(1)}, f32[14,8,128]{2,1,0:T(8,128)S(1)}, u32[]{:S(2)}, u32[]{:S(2)}) %collective-permute-start.1) | collective-permute-done | bytes 57376 | tf_op jit(solution)/shard_map/ppermute | solution.py:340
  29.9 3.9 %collective-permute-start.5 = (f32[28,8,128]{2,1,0:T(8,128)S(1)}, f32[28,8,128]{2,1,0:T(8,128)S(1)}, u32[]{:S(2)}, u32[]{:S(2)}) collective-permute-start(f32[28,8,128]{2,1,0:T(8,128)S(1)} %constant_dynamic-update-slice_fusion), channel_id=1, source_target_pairs={{0,15},{1,0},{2,1},{3,2},{4,3},{5,4},{6,5},{7,6},{8,7},{9,8},{10,9... | collective-permute-start | bytes 344072 | tf_op jit(solution)/shard_map/ppermute | solution.py:340
  33.9 1.9 %collective-permute-start.4 = (f32[28,8,128]{2,1,0:T(8,128)S(1)}, f32[28,8,128]{2,1,0:T(8,128)S(1)}, u32[]{:S(2)}, u32[]{:S(2)}) collective-permute-start(f32[28,8,128]{2,1,0:T(8,128)S(1)} %constant_dynamic-update-slice_fusion), channel_id=1, source_target_pairs={{0,1},{1,2},{2,3},{3,4},{4,5},{5,6},{6,7},{7,8},{8,9},{9,10},{10,1... | collective-permute-start | bytes 344072 | tf_op jit(solution)/shard_map/ppermute | solution.py:340
  35.8 0.0 collective-permute-done.5.cabove
  35.8 4.8 %collective-permute-done.4.cbelow = f32[28,8,128]{2,1,0:T(8,128)S(1)} collective-permute-done((f32[28,8,128]{2,1,0:T(8,128)S(1)}, f32[28,8,128]{2,1,0:T(8,128)S(1)}, u32[]{:S(2)}, u32[]{:S(2)}) %collective-permute-start.4) | collective-permute-done | bytes 114720 | tf_op jit(solution)/shard_map/ppermute | solution.py:340
  40.7 15.4 %advance.1 = (f32[3,16,8,128]{3,2,1,0:T(8,128)S(1)}, f32[16,8,128]{2,1,0:T(8,128)}, f32[3,16,8,128]{3,2,1,0:T(8,128)S(1)}, f32[3,16,8,128]{3,2,1,0:T(8,128)S(1)}...) custom-call(f32[3,16,8,128]{3,2,1,0:T(8,128)S(1)} %copy-done.1, f32[16,8,128]{2,1,0:T(8,128)S(1)} %copy-done.9, ...), custom_call_target="tpu_custom_call" | custom-call | tf_op jit(solution)/shard_map/advance/pallas_call | solution.py:368
  56.1 15.1 %all_to_all.17 = f32[32,1,128]{2,1,0:T(1,128)S(1)} all-to-all(f32[32,1,128]{2,1,0:T(1,128)S(1)} %bitcast.5), channel_id=1, replica_groups=mesh['gx'=32,'gy'=16] {'gx'}, dimensions={0} | all-to-all | bytes 32768 | tf_op jit(solution)/shard_map/all_to_all | solution.py:395
  71.2 0.1 reduce_sum.9
  71.3 18.0 %all_to_all.18 = f32[16,1,128]{2,1,0:T(1,128)S(1)} all-to-all(f32[16,1,128]{2,1,0:T(1,128)S(1)} %broadcast_in_dim.2), channel_id=1, replica_groups=mesh['gx'=32,'gy'=16] {'gy'}, dimensions={0} | all-to-all | bytes 16384 | tf_op jit(solution)/shard_map/all_to_all | solution.py:397
  89.3 0.9 combine.1
  (21 shorter events, 0.1 us)
Async XLA Ops:
  0.6 0.9 %copy-start = (f32[3,16,8,128]{3,2,1,0:T(8,128)S(1)}, f32[3,16,8,128]{3,2,1,0:T(8,128)}, u32[]{:S(2)}) copy-start(f32[3,16,8,128]{3,2,1,0:T(8,128)} %mom.3) | copy-start | bytes 589828
  1.6 0.9 %copy-start.2 = (f32[3,16,8,128]{3,2,1,0:T(8,128)S(1)}, f32[3,16,8,128]{3,2,1,0:T(8,128)}, u32[]{:S(2)}) copy-start(f32[3,16,8,128]{3,2,1,0:T(8,128)} %cou.3) | copy-start | bytes 589828
  2.5 0.9 %copy-start.4 = (f32[3,16,8,128]{3,2,1,0:T(8,128)S(1)}, f32[3,16,8,128]{3,2,1,0:T(8,128)}, u32[]{:S(2)}) copy-start(f32[3,16,8,128]{3,2,1,0:T(8,128)} %dia.3) | copy-start | bytes 589828
  3.4 0.9 %copy-start.6 = (f32[3,16,8,128]{3,2,1,0:T(8,128)S(1)}, f32[3,16,8,128]{3,2,1,0:T(8,128)}, u32[]{:S(2)}) copy-start(f32[3,16,8,128]{3,2,1,0:T(8,128)} %cro.3) | copy-start | bytes 589828
  4.3 0.8 copy-start.8
  5.2 0.8 copy-start.10
  6.0 34.6 %copy-start.3 = (f32[3,16,8,128]{3,2,1,0:T(8,128)S(1)}, f32[3,16,8,128]{3,2,1,0:T(8,128)}, u32[]{:S(2)}) copy-start(f32[3,16,8,128]{3,2,1,0:T(8,128)} %cou.3) | copy-start | bytes 589828
  6.0 34.6 %copy-start.5 = (f32[3,16,8,128]{3,2,1,0:T(8,128)S(1)}, f32[3,16,8,128]{3,2,1,0:T(8,128)}, u32[]{:S(2)}) copy-start(f32[3,16,8,128]{3,2,1,0:T(8,128)} %dia.3) | copy-start | bytes 589828
  6.0 34.6 %copy-start.7 = (f32[3,16,8,128]{3,2,1,0:T(8,128)S(1)}, f32[3,16,8,128]{3,2,1,0:T(8,128)}, u32[]{:S(2)}) copy-start(f32[3,16,8,128]{3,2,1,0:T(8,128)} %cro.3) | copy-start | bytes 589828
  6.0 34.6 %copy-start.9 = (f32[16,8,128]{2,1,0:T(8,128)S(1)}, f32[16,8,128]{2,1,0:T(8,128)}, u32[]{:S(2)}) copy-start(f32[16,8,128]{2,1,0:T(8,128)} %th.3) | copy-start | bytes 196612
  6.0 34.6 %copy-start.11 = (f32[16,8,128]{2,1,0:T(8,128)S(1)}, f32[16,8,128]{2,1,0:T(8,128)}, u32[]{:S(2)}) copy-start(f32[16,8,128]{2,1,0:T(8,128)} %den.3) | copy-start | bytes 196612
  6.3 34.3 %copy-start.1 = (f32[3,16,8,128]{3,2,1,0:T(8,128)S(1)}, f32[3,16,8,128]{3,2,1,0:T(8,128)}, u32[]{:S(2)}) copy-start(f32[3,16,8,128]{3,2,1,0:T(8,128)} %mom.3) | copy-start | bytes 589828
  6.4 34.3 %collective-permute-start.2 = (f32[7,16,8,128]{3,2,1,0:T(8,128)S(1)}, f32[7,16,8,128]{3,2,1,0:T(8,128)S(1)}, u32[]{:S(2)}, u32[]{:S(2)}) collective-permute-start(f32[7,16,8,128]{3,2,1,0:T(8,128)S(1)} %get-tuple-element.17), channel_id=1, source_target_pairs={{0,1},{1,2},{2,3},{3,4},{4,5},{5,6},{6,7},{7,8},{8,9},{9,10},{10,1... | collective-permute-start | bytes 1376264 | tf_op jit(solution)/shard_map/ppermute | solution.py:340
  10.9 29.7 %collective-permute-start.3 = (f32[7,16,8,128]{3,2,1,0:T(8,128)S(1)}, f32[7,16,8,128]{3,2,1,0:T(8,128)S(1)}, u32[]{:S(2)}, u32[]{:S(2)}) collective-permute-start(f32[7,16,8,128]{3,2,1,0:T(8,128)S(1)} %get-tuple-element.18), channel_id=1, source_target_pairs={{0,15},{1,0},{2,1},{3,2},{4,3},{5,4},{6,5},{7,6},{8,7},{9,8},{10,9... | collective-permute-start | bytes 1376264 | tf_op jit(solution)/shard_map/ppermute | solution.py:340
  20.4 6.0 %collective-permute-start = (f32[14,8,128]{2,1,0:T(8,128)S(1)}, f32[14,8,128]{2,1,0:T(8,128)S(1)}, u32[]{:S(2)}, u32[]{:S(2)}) collective-permute-start(f32[14,8,128]{2,1,0:T(8,128)S(1)} %get-tuple-element.15), channel_id=1, source_target_pairs={{0,16},{16,32},{32,48},{48,64},{64,80},{80,96},{96,112},{112,128},... | collective-permute-start | bytes 172040 | tf_op jit(solution)/shard_map/ppermute | solution.py:340
  24.4 5.5 %collective-permute-start.1 = (f32[14,8,128]{2,1,0:T(8,128)S(1)}, f32[14,8,128]{2,1,0:T(8,128)S(1)}, u32[]{:S(2)}, u32[]{:S(2)}) collective-permute-start(f32[14,8,128]{2,1,0:T(8,128)S(1)} %get-tuple-element.16), channel_id=1, source_target_pairs={{0,496},{16,0},{32,16},{48,32},{64,48},{80,64},{96,80},{112,96},{1... | collective-permute-start | bytes 172040 | tf_op jit(solution)/shard_map/ppermute | solution.py:340
  29.9 5.9 %collective-permute-start.5 = (f32[28,8,128]{2,1,0:T(8,128)S(1)}, f32[28,8,128]{2,1,0:T(8,128)S(1)}, u32[]{:S(2)}, u32[]{:S(2)}) collective-permute-start(f32[28,8,128]{2,1,0:T(8,128)S(1)} %constant_dynamic-update-slice_fusion), channel_id=1, source_target_pairs={{0,15},{1,0},{2,1},{3,2},{4,3},{5,4},{6,5},{7,6},{8,7},{9,8},{10,9... | collective-permute-start | bytes 344072 | tf_op jit(solution)/shard_map/ppermute | solution.py:340
  33.9 6.7 %collective-permute-start.4 = (f32[28,8,128]{2,1,0:T(8,128)S(1)}, f32[28,8,128]{2,1,0:T(8,128)S(1)}, u32[]{:S(2)}, u32[]{:S(2)}) collective-permute-start(f32[28,8,128]{2,1,0:T(8,128)S(1)} %constant_dynamic-update-slice_fusion), channel_id=1, source_target_pairs={{0,1},{1,2},{2,3},{3,4},{4,5},{5,6},{6,7},{7,8},{8,9},{9,10},{10,1... | collective-permute-start | bytes 344072 | tf_op jit(solution)/shard_map/ppermute | solution.py:340

commit v2 on v1

--- a/solution.py
+++ b/solution.py
@@ -59,9 +59,15 @@
     return cro.at[f - 11]
 
 
-def pack_kernel(mom, th, cou, den, dia, cro, to_left, to_right, to_up, to_down):
-    refs = (mom, th, cou, den, dia, cro)
-    nz = den.shape[0]
+def pack_kernel(*refs):
+    sources, (to_left, to_right, to_up, to_down) = refs[:6], refs[6:10]
+    refs, sem = refs[10:16], refs[16]
+    copies = [pltpu.make_async_copy(a, b, sem.at[i]) for i, (a, b) in enumerate(zip(sources, refs))]
+    for copy in copies:
+        copy.start()
+    for copy in copies:
+        copy.wait()
+    nz = refs[1].shape[0]
     lane = lanes((8, 128)) // 8
     row = rows((8, 128))
     for f in range(NF):
@@ -155,7 +161,7 @@
             out.append(up)
         return tuple(out)
 
-    lax.fori_loop(1, nz + 1, upwind, (zero,) * 4)
+    lax.fori_loop(1, nz + 1, upwind, (zero,) * 4, unroll=4)
     for f in range(4):
         P1[f, 0] = zero
         P1[f, nz + 1] = zero
@@ -184,7 +190,7 @@
             out.append(up)
         return tuple(out)
 
-    lax.fori_loop(1, nz + 1, anti, (zero,) * 4)
+    lax.fori_loop(1, nz + 1, anti, (zero,) * 4, unroll=4)
     M[2, 0] = zero
     M[2, nz + 1] = zero
 
@@ -212,7 +218,7 @@
         C[9, k] = 0.25 * S[A23, k]
         return carry
 
-    lax.fori_loop(1, nz + 1, first, 0)
+    lax.fori_loop(1, nz + 1, first, 0, unroll=4)
     for i in range(3):
         VV[i, 0] = zero
         VV[i, nz + 1] = zero
@@ -246,7 +252,7 @@
                 T[k] = t
             return carry
 
-        lax.fori_loop(1, nz + 1, flat, 0)
+        lax.fori_loop(1, nz + 1, flat, 0, unroll=4)
 
         pairs = [(j, i + 1) for j in range(i + 2)]
 
@@ -259,7 +265,8 @@
             vs = [own(VV[j, k]) for j in range(i + 1)] + [v]
             return tuple(s + vs[j] * v for s, (j, _) in zip(acc, pairs))
 
-        acc = lax.fori_loop(1, nz + 1, deep, (jnp.zeros((8, 128), F32),) * len(pairs))
+        start = (jnp.zeros((8, 128), F32),) * len(pairs)
+        acc = lax.fori_loop(1, nz + 1, deep, start, unroll=4)
         for s, key in zip(acc, pairs):
             sums[key] = s
     line = lanes((1, 128))
@@ -349,11 +356,12 @@
     to_left, to_right, to_up, to_down = pl.pallas_call(
         pack_kernel,
         out_shape=(sds((NF, 8, 128), F32),) * 2 + (sds((nc, nz, 8, 128), F32),) * 2,
-        in_specs=[vm] * 6,
+        in_specs=[pl.BlockSpec(memory_space=pltpu.HBM)] * 6,
         out_specs=[vm] * 4,
+        scratch_shapes=[pltpu.VMEM(a.shape, F32) for a in args] + [pltpu.SemaphoreType.DMA((6,))],
         compiler_params=pltpu.CompilerParams(vmem_limit_bytes=16 << 20),
         name="pack",
-    )(*args)
+    )(*(pltpu.with_memory_space_constraint(a, pltpu.HBM) for a in args))
     from_left = shift_to(to_right, "gx", 1)
     from_right = shift_to(to_left, "gx", -1)
     below = shift_to(to_up, "gy", 1)

time: 90.7 us -> 80.9 us (0.89)
  local copies, waits for them, and re-layouts: 5.42 us -> 0.05 us
  Pallas kernels: 16.6 us -> 12.4 us
    pallas_call x1, Pallas kernels: 15.4 us -> 9.83 us  [local(): pl.pallas_call(main_kernel, out_shape=(sds((3,) + block, F32), sds(block,...]
    unnamed x25 -> x13, local copies, waits for them, and re-layouts: 5.41 us -> 0.03 us
    pallas_call x1, Pallas kernels: 0.3 us -> 1.66 us  [local(): pl.pallas_call(pack_kernel, out_shape=(sds((NF, 8, 128), F32),) * 2 + (sd...]
where the time goes in v2:
time: 80.9 us; the launch traced here: 80.5 us
  blocking collectives  33.1 us (41%)
  starting transfers between devices  25.8 us (32%)
  Pallas kernels  12.4 us (15%)
  waiting for transfers between devices  8.36 us (10%)
  between operations  0.81 us (1%)
    ppermute x6, starting transfers between devices, shift_to(): return lax.ppermute(a, axis, [(i, (i + step) % n) for i in range(n)])  25.8 us
    all_to_all x1, blocking collectives, local(): part = lax.all_to_all(part, 'gy', 0, 0, tiled=True)  18 us
    all_to_all x1, blocking collectives, local(): part = lax.all_to_all(gram, 'gx', 0, 0, tiled=True)  15.1 us
    pallas_call x1, Pallas kernels, local(): pl.pallas_call(main_kernel, out_shape=(sds((3,) + block, F32), sds(block,...  9.83 us
    ppermute x6, waiting for transfers between devices, shift_to(): return lax.ppermute(a, axis, [(i, (i + step) % n) for i in range(n)])  8.36 us
    pallas_call x1, Pallas kernels, local(): pl.pallas_call(pack_kernel, out_shape=(sds((NF, 8, 128), F32),) * 2 + (sd...  1.66 us
  transfers between devices with their start and end apart: 6, of which 2 were waited for; matrix products, arithmetic and copies ran while one was open for 0% of the time, Pallas kernels for 0%

profile of v2, /device:TPU:1, one launch (start us, length us, event | category | flops | bytes accessed | tf_op | source)
XLA Modules:
  0.0 80.5 jit_solution(4761984775218917745)
XLA Ops:
  0.7 1.7 %pack.1 = (f32[14,8,128]{2,1,0:T(8,128)S(1)}, f32[14,8,128]{2,1,0:T(8,128)S(1)}, f32[7,16,8,128]{3,2,1,0:T(8,128)S(1)}, f32[7,16,8,128]{3,2,1,0:T(8,128)S(1)}) custom-call(f32[3,16,8,128]{3,2,1,0:T(8,128)} %mom.1, f32[16,8,128]{2,1,0:T(8,128)} %th.1, f32[3,16,8,128]{3,2,1,0:T(8,128)} %cou.1, f32[16,8,128]{2,1,0:T(8,128)} %den.1, f32[3,16,8,128]{3,2,1,0:T(8,128)} %dia.1, ...), custom_call_target="tpu_custom_call" | custom-call | tf_op jit(solution)/shard_map/pack/pallas_call | solution.py:356
  2.4 0.0 copy-start
  2.4 4.5 %collective-permute-start.2 = (f32[7,16,8,128]{3,2,1,0:T(8,128)S(1)}, f32[7,16,8,128]{3,2,1,0:T(8,128)S(1)}, u32[]{:S(2)}, u32[]{:S(2)}) collective-permute-start(f32[7,16,8,128]{3,2,1,0:T(8,128)S(1)} %get-tuple-element.17), channel_id=1, source_target_pairs={{0,1},{1,2},{2,3},{3,4},{4,5},{5,6},{6,7},{7,8},{8,9},{9,10},{10,1... | collective-permute-start | bytes 1376264 | tf_op jit(solution)/shard_map/ppermute | solution.py:347
  6.9 9.5 %collective-permute-start.3 = (f32[7,16,8,128]{3,2,1,0:T(8,128)S(1)}, f32[7,16,8,128]{3,2,1,0:T(8,128)S(1)}, u32[]{:S(2)}, u32[]{:S(2)}) collective-permute-start(f32[7,16,8,128]{3,2,1,0:T(8,128)S(1)} %get-tuple-element.18), channel_id=1, source_target_pairs={{0,15},{1,0},{2,1},{3,2},{4,3},{5,4},{6,5},{7,6},{8,7},{9,8},{10,9... | collective-permute-start | bytes 1376264 | tf_op jit(solution)/shard_map/ppermute | solution.py:347
  16.4 4.0 %collective-permute-start = (f32[14,8,128]{2,1,0:T(8,128)S(1)}, f32[14,8,128]{2,1,0:T(8,128)S(1)}, u32[]{:S(2)}, u32[]{:S(2)}) collective-permute-start(f32[14,8,128]{2,1,0:T(8,128)S(1)} %get-tuple-element.15), channel_id=1, source_target_pairs={{0,16},{16,32},{32,48},{48,64},{64,80},{80,96},{96,112},{112,128},... | collective-permute-start | bytes 172040 | tf_op jit(solution)/shard_map/ppermute | solution.py:347
  20.4 1.9 %collective-permute-start.1 = (f32[14,8,128]{2,1,0:T(8,128)S(1)}, f32[14,8,128]{2,1,0:T(8,128)S(1)}, u32[]{:S(2)}, u32[]{:S(2)}) collective-permute-start(f32[14,8,128]{2,1,0:T(8,128)S(1)} %get-tuple-element.16), channel_id=1, source_target_pairs={{0,496},{16,0},{32,16},{48,32},{64,48},{80,64},{96,80},{112,96},{1... | collective-permute-start | bytes 172040 | tf_op jit(solution)/shard_map/ppermute | solution.py:347
  22.4 0.0 collective-permute-done.from_left
  22.4 3.5 %collective-permute-done.1.from_right = f32[14,8,128]{2,1,0:T(8,128)S(1)} collective-permute-done((f32[14,8,128]{2,1,0:T(8,128)S(1)}, f32[14,8,128]{2,1,0:T(8,128)S(1)}, u32[]{:S(2)}, u32[]{:S(2)}) %collective-permute-start.1) | collective-permute-done | bytes 57376 | tf_op jit(solution)/shard_map/ppermute | solution.py:347
  25.9 3.9 %collective-permute-start.5 = (f32[28,8,128]{2,1,0:T(8,128)S(1)}, f32[28,8,128]{2,1,0:T(8,128)S(1)}, u32[]{:S(2)}, u32[]{:S(2)}) collective-permute-start(f32[28,8,128]{2,1,0:T(8,128)S(1)} %constant_dynamic-update-slice_fusion), channel_id=1, source_target_pairs={{0,15},{1,0},{2,1},{3,2},{4,3},{5,4},{6,5},{7,6},{8,7},{9,8},{10,9... | collective-permute-start | bytes 344072 | tf_op jit(solution)/shard_map/ppermute | solution.py:347
  29.9 1.9 %collective-permute-start.4 = (f32[28,8,128]{2,1,0:T(8,128)S(1)}, f32[28,8,128]{2,1,0:T(8,128)S(1)}, u32[]{:S(2)}, u32[]{:S(2)}) collective-permute-start(f32[28,8,128]{2,1,0:T(8,128)S(1)} %constant_dynamic-update-slice_fusion), channel_id=1, source_target_pairs={{0,1},{1,2},{2,3},{3,4},{4,5},{5,6},{6,7},{7,8},{8,9},{9,10},{10,1... | collective-permute-start | bytes 344072 | tf_op jit(solution)/shard_map/ppermute | solution.py:347
  31.8 0.0 collective-permute-done.5.cabove
  31.8 4.8 %collective-permute-done.4.cbelow = f32[28,8,128]{2,1,0:T(8,128)S(1)} collective-permute-done((f32[28,8,128]{2,1,0:T(8,128)S(1)}, f32[28,8,128]{2,1,0:T(8,128)S(1)}, u32[]{:S(2)}, u32[]{:S(2)}) %collective-permute-start.4) | collective-permute-done | bytes 114720 | tf_op jit(solution)/shard_map/ppermute | solution.py:347
  36.6 0.0 collective-permute-done.2.below
  36.6 0.0 collective-permute-done.3.above
  36.6 0.0 copy-done.2
  36.6 0.0 copy-done.3
  36.7 0.0 copy-done.4
  36.7 0.0 copy-done.5
  36.7 0.0 copy-done
  36.7 9.8 %advance.1 = (f32[3,16,8,128]{3,2,1,0:T(8,128)S(1)}, f32[16,8,128]{2,1,0:T(8,128)}, f32[3,16,8,128]{3,2,1,0:T(8,128)S(1)}, f32[3,16,8,128]{3,2,1,0:T(8,128)S(1)}...) custom-call(f32[3,16,8,128]{3,2,1,0:T(8,128)S(1)} %copy-done, f32[16,8,128]{2,1,0:T(8,128)S(1)} %copy-done.4, ...), custom_call_target="tpu_custom_call" | custom-call | tf_op jit(solution)/shard_map/advance/pallas_call | solution.py:376
  46.5 15.1 %all_to_all.17 = f32[32,1,128]{2,1,0:T(1,128)S(1)} all-to-all(f32[32,1,128]{2,1,0:T(1,128)S(1)} %bitcast.5), channel_id=1, replica_groups=mesh['gx'=32,'gy'=16] {'gx'}, dimensions={0} | all-to-all | bytes 32768 | tf_op jit(solution)/shard_map/all_to_all | solution.py:403
  61.6 0.1 reduce_sum.9
  61.6 18.0 %all_to_all.18 = f32[16,1,128]{2,1,0:T(1,128)S(1)} all-to-all(f32[16,1,128]{2,1,0:T(1,128)S(1)} %broadcast_in_dim.2), channel_id=1, replica_groups=mesh['gx'=32,'gy'=16] {'gy'}, dimensions={0} | all-to-all | bytes 16384 | tf_op jit(solution)/shard_map/all_to_all | solution.py:405
  79.7 0.9 %combine.1 = (f32[3,16,8,128]{3,2,1,0:T(8,128)}, f32[16,8,128]{2,1,0:T(8,128)}) custom-call(f32[16,128]{1,0:T(8,128)S(1)} %bitcast.4, f32[3,16,8,128]{3,2,1,0:T(8,128)S(1)} %get-tuple-element.20.moved, f32[3,16,8,128]{3,2,1,0:T(8,128)S(1)} %get-tuple-element.21.basis, f32[3,16,8,128]{3,2,1,0:T(8,128)S(1)} %get-tuple-element.22.dxs, ...), custom_call_target="tpu_custom_call" | custom-call | tf_op jit(solution)/shard_map/combine/pallas_call | solution.py:407
  (9 shorter events, 0.0 us)
Async XLA Ops:
  0.6 36.0 %copy-start.1 = (f32[3,16,8,128]{3,2,1,0:T(8,128)S(1)}, f32[3,16,8,128]{3,2,1,0:T(8,128)}, u32[]{:S(2)}) copy-start(f32[3,16,8,128]{3,2,1,0:T(8,128)} %cou.1) | copy-start | bytes 589828
  0.6 36.0 %copy-start.2 = (f32[3,16,8,128]{3,2,1,0:T(8,128)S(1)}, f32[3,16,8,128]{3,2,1,0:T(8,128)}, u32[]{:S(2)}) copy-start(f32[3,16,8,128]{3,2,1,0:T(8,128)} %dia.1) | copy-start | bytes 589828
  0.7 36.0 %copy-start.3 = (f32[3,16,8,128]{3,2,1,0:T(8,128)S(1)}, f32[3,16,8,128]{3,2,1,0:T(8,128)}, u32[]{:S(2)}) copy-start(f32[3,16,8,128]{3,2,1,0:T(8,128)} %cro.1) | copy-start | bytes 589828
  0.7 36.0 %copy-start.4 = (f32[16,8,128]{2,1,0:T(8,128)S(1)}, f32[16,8,128]{2,1,0:T(8,128)}, u32[]{:S(2)}) copy-start(f32[16,8,128]{2,1,0:T(8,128)} %th.1) | copy-start | bytes 196612
  0.7 36.0 %copy-start.5 = (f32[16,8,128]{2,1,0:T(8,128)S(1)}, f32[16,8,128]{2,1,0:T(8,128)}, u32[]{:S(2)}) copy-start(f32[16,8,128]{2,1,0:T(8,128)} %den.1) | copy-start | bytes 196612
  2.4 34.3 %copy-start = (f32[3,16,8,128]{3,2,1,0:T(8,128)S(1)}, f32[3,16,8,128]{3,2,1,0:T(8,128)}, u32[]{:S(2)}) copy-start(f32[3,16,8,128]{3,2,1,0:T(8,128)} %mom.1) | copy-start | bytes 589828
  2.4 34.3 %collective-permute-start.2 = (f32[7,16,8,128]{3,2,1,0:T(8,128)S(1)}, f32[7,16,8,128]{3,2,1,0:T(8,128)S(1)}, u32[]{:S(2)}, u32[]{:S(2)}) collective-permute-start(f32[7,16,8,128]{3,2,1,0:T(8,128)S(1)} %get-tuple-element.17), channel_id=1, source_target_pairs={{0,1},{1,2},{2,3},{3,4},{4,5},{5,6},{6,7},{7,8},{8,9},{9,10},{10,1... | collective-permute-start | bytes 1376264 | tf_op jit(solution)/shard_map/ppermute | solution.py:347
  6.9 29.7 %collective-permute-start.3 = (f32[7,16,8,128]{3,2,1,0:T(8,128)S(1)}, f32[7,16,8,128]{3,2,1,0:T(8,128)S(1)}, u32[]{:S(2)}, u32[]{:S(2)}) collective-permute-start(f32[7,16,8,128]{3,2,1,0:T(8,128)S(1)} %get-tuple-element.18), channel_id=1, source_target_pairs={{0,15},{1,0},{2,1},{3,2},{4,3},{5,4},{6,5},{7,6},{8,7},{9,8},{10,9... | collective-permute-start | bytes 1376264 | tf_op jit(solution)/shard_map/ppermute | solution.py:347
  16.4 6.0 %collective-permute-start = (f32[14,8,128]{2,1,0:T(8,128)S(1)}, f32[14,8,128]{2,1,0:T(8,128)S(1)}, u32[]{:S(2)}, u32[]{:S(2)}) collective-permute-start(f32[14,8,128]{2,1,0:T(8,128)S(1)} %get-tuple-element.15), channel_id=1, source_target_pairs={{0,16},{16,32},{32,48},{48,64},{64,80},{80,96},{96,112},{112,128},... | collective-permute-start | bytes 172040 | tf_op jit(solution)/shard_map/ppermute | solution.py:347
  20.4 5.5 %collective-permute-start.1 = (f32[14,8,128]{2,1,0:T(8,128)S(1)}, f32[14,8,128]{2,1,0:T(8,128)S(1)}, u32[]{:S(2)}, u32[]{:S(2)}) collective-permute-start(f32[14,8,128]{2,1,0:T(8,128)S(1)} %get-tuple-element.16), channel_id=1, source_target_pairs={{0,496},{16,0},{32,16},{48,32},{64,48},{80,64},{96,80},{112,96},{1... | collective-permute-start | bytes 172040 | tf_op jit(solution)/shard_map/ppermute | solution.py:347
  25.9 5.9 %collective-permute-start.5 = (f32[28,8,128]{2,1,0:T(8,128)S(1)}, f32[28,8,128]{2,1,0:T(8,128)S(1)}, u32[]{:S(2)}, u32[]{:S(2)}) collective-permute-start(f32[28,8,128]{2,1,0:T(8,128)S(1)} %constant_dynamic-update-slice_fusion), channel_id=1, source_target_pairs={{0,15},{1,0},{2,1},{3,2},{4,3},{5,4},{6,5},{7,6},{8,7},{9,8},{10,9... | collective-permute-start | bytes 344072 | tf_op jit(solution)/shard_map/ppermute | solution.py:347
  29.9 6.7 %collective-permute-start.4 = (f32[28,8,128]{2,1,0:T(8,128)S(1)}, f32[28,8,128]{2,1,0:T(8,128)S(1)}, u32[]{:S(2)}, u32[]{:S(2)}) collective-permute-start(f32[28,8,128]{2,1,0:T(8,128)S(1)} %constant_dynamic-update-slice_fusion), channel_id=1, source_target_pairs={{0,1},{1,2},{2,3},{3,4},{4,5},{5,6},{6,7},{7,8},{8,9},{9,10},{10,1... | collective-permute-start | bytes 344072 | tf_op jit(solution)/shard_map/ppermute | solution.py:347

commit v3 on v2

v3 whole, which is shorter than its diff:
```python
import jax
import jax.numpy as jnp
from jax import lax
from jax.experimental import pallas as pl
from jax.experimental.pallas import tpu as pltpu
from jax.sharding import PartitionSpec as P

helm = 0.02
ITERS = 3
NF = 14
U, V, W, TH, G, CX, CY, CZ, A11, A22, A33, A12, A13, A23 = range(NF)
COMBOS = (
    (V, 6, TH, 2),
    (CY, 6, A12, 2),
    (U, 5, A22, 3),
    (W, 5, A11, 2),
    (G, 5, A33, 2),
    (CX, 5, A13, 2),
    (CZ, 5, A23, 2),
)
F32 = jnp.float32


def lanes(shape):
    return lax.broadcasted_iota(jnp.int32, shape, len(shape) - 1)


def rows(shape):
    return lax.broadcasted_iota(jnp.int32, shape, len(shape) - 2)


def roll(a, shift, axis):
    shift = shift % a.shape[axis]
    if shift == 0:
        return a
    return pltpu.roll(a, shift, axis)


def xs(a, d):
    return roll(a, -d, 1)


def ys(a, d):
    return roll(a, -d, 0)


def rim_x(q, d):
    c = lanes((48, 128)) % 8
    moved = roll(q, -d, 1)
    if d > 0:
        first = jnp.where(c == 7, roll(q[48:], 7, 1), moved[:48])
        return jnp.concatenate((first, moved[48:]), axis=0)
    last = jnp.where(c == 0, roll(q[:48], -7, 1), moved[48:])
    return jnp.concatenate((moved[:48], last), axis=0)


def rim_z(q, d):
    lane = lanes(q.shape)
    end = lane >= 120 if d > 0 else lane < 8
    return jnp.where(end, 0.0, roll(q, -8 * d, 1))


def rim_own(q):
    return jnp.where(lanes((8, 128)) % 8 < 4, q[56:64], q[32:40])


def upwind_weights(cx, cr, cy, cd, cz, cu, dens):
    ig = 1.0 / dens
    pos, neg = (lambda a: jnp.maximum(a, 0.0)), (lambda a: jnp.minimum(a, 0.0))
    rp, rn, lp, ln = pos(cr), neg(cr), pos(cx), neg(cx)
    dp, dn, up, un = pos(cd), neg(cd), pos(cy), neg(cy)
    ap, an, bp, bn = pos(cu), neg(cu), pos(cz), neg(cz)
    mid = 1.0 - ig * (((rp - ln) + (dp - un)) + (ap - bn))
    return mid, tuple(ig * a for a in (lp, -rn, up, -dn, bp, -an)), ig


def face(c, one, two):
    return 0.5 * (jnp.abs(c) - c * c / (0.5 * (one + two)))


def anti_weights(faces, ig):
    kl, kr, ku, kd, kb, ka = faces
    mid = 1.0 + ig * (((kl + kr) + (ku + kd)) + (ka + kb))
    return mid, tuple(-ig * a for a in faces)


def seven(mid, w, p, around):
    x = w[0] * around[0] + w[1] * around[1]
    y = w[2] * around[2] + w[3] * around[3]
    z = w[4] * around[4] + w[5] * around[5]
    return (mid * p + x) + (y + z)


def field_of(refs, f):
    mom, th, cou, den, dia, cro = refs
    if f < 3:
        return mom.at[f]
    if f == TH:
        return th
    if f == G:
        return den
    if f < 8:
        return cou.at[f - 5]
    if f < 11:
        return dia.at[f - 8]
    return cro.at[f - 11]


def fetch_kernel(*refs):
    sources, refs, (to_up, to_down, sem) = refs[:6], refs[6:12], refs[12:]
    copies = [pltpu.make_async_copy(a, b, sem.at[i]) for i, (a, b) in enumerate(zip(sources, refs))]
    for copy in copies:
        copy.start()
    for copy in copies:
        copy.wait()
    cou = refs[2]
    nz = refs[1].shape[0]
    row = rows((8, 128))
    first_row = (row == 0) & (lax.axis_index("gy") == 0)
    for k in range(nz):
        cou[1, k] = jnp.where(first_row, 0.0, cou[1, k])
    cou[2, 0] = jnp.zeros((8, 128), F32)
    for c, (first, n, second, m) in enumerate(COMBOS):
        one, two = field_of(refs, first), field_of(refs, second)
        for k in range(nz):
            a, b = one[k], two[k]
            to_down[c, k] = jnp.where(row < n, a, roll(b, n, 0))
            to_up[c, k] = jnp.where(row >= 8 - n, a, roll(b, -n, 0))


def strips_kernel(mom, th, cou, den, dia, cro, below, above, S, to_left, to_right):
    refs = (mom, th, cou, den, dia, cro)
    nz = den.shape[0]
    gy = lax.axis_index("gy")
    has_below = gy > 0
    has_above = gy < lax.axis_size("gy") - 1
    slot = lanes((24, 128)) // 8
    for c, (first, n, second, m) in enumerate(COMBOS):
        for f, shift in ((first, 0), (second, n)):
            ref = field_of(refs, f)
            outside = 1.0 if f == G else 0.0
            left = jnp.zeros((24, 128), F32)
            right = jnp.zeros((24, 128), F32)
            for k in range(nz):
                low = jnp.where(has_below, roll(below[c, k], shift, 0), outside)
                high = jnp.where(has_above, roll(above[c, k], -shift, 0), outside)
                whole = jnp.concatenate((low, ref[k], high), axis=0)
                S[f, k + 1] = whole
                moved = roll(whole, 8 * k, 1)
                left = jnp.where(slot == k, moved, left)
                right = jnp.where(slot == (k - 1) % nz, moved, right)
            to_left[f] = left
            to_right[f] = roll(right, 8, 1)
            pad = jnp.full((24, 128), outside, F32)
            S[f, 0] = pad
            S[f, nz + 1] = pad


def masks(shape):
    gy = lax.axis_index("gy")
    has_below = gy > 0
    has_above = gy < lax.axis_size("gy") - 1
    row = rows(shape) % 24
    inside = ((row >= 8) | has_below) & ((row < 16) | has_above)
    edge = ((row == 8) & ~has_below) | ((row == 16) & ~has_above)
    return inside, edge


def core_kernel(S, moved, right_side, C, P1, M):
    nz = moved.shape[1]
    shape = (24, 128)
    inside, edge = masks(shape)
    zero = jnp.zeros(shape, F32)

    def upwind(k, carry):
        cx, cy, cz, cu = S[CX, k], S[CY, k], S[CZ, k], S[CZ, k + 1]
        mid, w, ig = upwind_weights(cx, xs(cx, 1), cy, ys(cy, 1), cz, cu, S[G, k])
        for f in range(4):
            psi = S[f, k]
            around = (xs(psi, -1), xs(psi, 1), ys(psi, -1), ys(psi, 1), S[f, k - 1], S[f, k + 1])
            P1[f, k] = seven(mid, w, psi, around)
        return carry

    lax.fori_loop(1, nz + 1, upwind, 0, unroll=4)
    for f in range(4):
        P1[f, 0] = zero
        P1[f, nz + 1] = zero

    def anti(k, kb):
        dens = S[G, k]
        kl = face(S[CX, k], xs(dens, -1), dens)
        ku = face(S[CY, k], ys(dens, -1), dens)
        ka = face(S[CZ, k + 1], dens, S[G, k + 1])
        mid, w = anti_weights((kl, xs(kl, 1), ku, ys(ku, 1), kb, ka), 1.0 / dens)
        for f in range(4):
            psi = P1[f, k]
            around = (xs(psi, -1), xs(psi, 1), ys(psi, -1), ys(psi, 1), P1[f, k - 1], P1[f, k + 1])
            res = seven(mid, w, psi, around)
            if f < 3:
                M[f, k] = res
            moved[f, k - 1] = res[8:16]
        return ka

    lax.fori_loop(1, nz + 1, anti, zero, unroll=4)
    M[2, 0] = zero
    M[2, nz + 1] = zero

    def first(k, carry):
        u, v = M[0, k], M[1, k]
        rhs = 0.5 * (
            (xs(u, 1) - xs(u, -1)) + (ys(v, 1) - ys(v, -1)) + (M[2, k + 1] - M[2, k - 1])
        )
        right_side[k - 1] = jnp.where(inside, rhs, 0.0)
        a11, a22, a33 = S[A11, k], S[A22, k], S[A33, k]
        wxl = 0.5 * (xs(a11, -1) + a11)
        wyl = jnp.where(edge, 0.0, 0.5 * (ys(a22, -1) + a22))
        wzl = jnp.where(k > 1, 0.5 * (S[A33, k - 1] + a33), 0.0)
        wz = jnp.where(k < nz, 0.5 * (S[A33, k + 1] + a33), 0.0)
        wx, wy = xs(wxl, 1), ys(wyl, 1)
        for n, w in enumerate((wx, wxl, wy, wyl, wz, wzl)):
            C[n, k - 1] = w
        C[6, k - 1] = ((wx + wxl) + (wy + wyl)) + ((wz + wzl) + helm)
        C[7, k - 1] = 0.25 * S[A12, k]
        C[8, k - 1] = 0.25 * S[A13, k]
        C[9, k - 1] = 0.25 * S[A23, k]
        return carry

    lax.fori_loop(1, nz + 1, first, 0, unroll=4)


def solve_kernel(
    right_side, C, to_left, to_right, from_left, from_right,
    basis, dxs, dys, rim_moved, rim_basis, rim_dxs, rim_dys, gram,
    VV, D, E, T,
):
    nz = right_side.shape[0]
    shape = (24, 128)
    zero = jnp.zeros(shape, F32)
    inside, edge = masks((96, 128))
    lane96 = lanes((96, 128))

    def rim_field(f):
        return jnp.concatenate((from_left[f], to_right[f], to_left[f], from_right[f]), axis=0)

    def around(q):
        return (
            rim_x(q, -1), rim_x(q, 1), ys(q, -1), ys(q, 1), rim_z(q, -1), rim_z(q, 1)
        )

    cx, cy, cz, dens = rim_field(CX), rim_field(CY), rim_field(CZ), rim_field(G)
    cu = rim_z(cz, 1)
    mid, w, ig = upwind_weights(cx, rim_x(cx, 1), cy, ys(cy, 1), cz, cu, dens)
    kl = face(cx, rim_x(dens, -1), dens)
    ku = face(cy, ys(dens, -1), dens)
    kb = face(cz, roll(dens, 8, 1), dens)
    mid2, w2 = anti_weights((kl, rim_x(kl, 1), ku, ys(ku, 1), kb, rim_z(kb, 1)), ig)
    done = []
    for f in range(4):
        psi = rim_field(f)
        psi = seven(mid, w, psi, around(psi))
        psi = seven(mid2, w2, psi, around(psi))
        rim_moved[f] = rim_own(psi)
        done.append(psi)
    u, v, t = done[:3]
    v0 = 0.5 * (
        (rim_x(u, 1) - rim_x(u, -1)) + (ys(v, 1) - ys(v, -1)) + (rim_z(t, 1) - rim_z(t, -1))
    )
    v0 = jnp.where(inside, v0, 0.0)

    lane = lanes(shape)
    c24 = lane % 8
    slot = lane // 8
    edges = jnp.where(c24 < 4, v0[48:72], v0[24:48])
    turned = [roll(edges, -8 * k, 1) for k in range(nz)]
    inner = zero
    for k in range(nz):
        core = right_side[k]
        VV[0, k + 1] = jnp.where(
            lane < 4, turned[k], jnp.where(lane >= 124, turned[(k + 1) % nz], core)
        )
        take = ((slot == k) & (c24 >= 4)) | ((slot == (k - 1) % nz) & (c24 < 4))
        inner = jnp.where(take, roll(core, 8 * k, 1), inner)
    q = jnp.concatenate(
        (
            v0[0:24],
            jnp.where(c24 < 4, roll(inner, 8, 1), v0[24:48]),
            jnp.where(c24 >= 4, inner, v0[48:72]),
            v0[72:96],
        ),
        axis=0,
    )

    a11, a22, a33 = rim_field(A11), rim_field(A22), rim_field(A33)
    wxl = 0.5 * (rim_x(a11, -1) + a11)
    wyl = jnp.where(edge, 0.0, 0.5 * (ys(a22, -1) + a22))
    wzl = jnp.where(lane96 < 8, 0.0, 0.5 * (roll(a33, 8, 1) + a33))
    wx, wy, wz = rim_x(wxl, 1), ys(wyl, 1), rim_z(wzl, 1)
    wc = ((wx + wxl) + (wy + wyl)) + ((wz + wzl) + helm)
    q12, q13, q23 = (0.25 * rim_field(f) for f in (A12, A13, A23))
    rims = [rim_own(q)]
    rim_basis[0] = rims[0]
    for i in range(3):
        xm, xp, ym, yp, zm, zp = around(q)
        d, e = xp - xm, yp - ym
        rim_dxs[i] = rim_own(d)
        rim_dys[i] = rim_own(e)
        new = seven(-wc, (wxl, wx, wyl, wy, wzl, wz), q, (xm, xp, ym, yp, zm, zp))
        new = new + q12 * (ys(d, 1) - ys(d, -1))
        new = new + q13 * (rim_z(d, 1) - rim_z(d, -1))
        q = new + q23 * (rim_z(e, 1) - rim_z(e, -1))
        rims.append(rim_own(q))
        if i < 2:
            rim_basis[i + 1] = rims[-1]

    for i in range(3):
        VV[i, 0] = zero
        VV[i, nz + 1] = zero
    for a in (D, E):
        a[0] = zero
        a[nz + 1] = zero
    own = lambda a: a[8:16]
    sums = {}
    for i in range(3):
        last = i == 2
        cut = own if last else (lambda a: a)

        def flat(k, carry, i=i, cut=cut, last=last):
            p = VV[i, k]
            xp, xm, yp, ym = xs(p, 1), xs(p, -1), ys(p, 1), ys(p, -1)
            d, e = xp - xm, yp - ym
            D[k] = d
            E[k] = e
            dxs[i, k - 1] = own(d)
            dys[i, k - 1] = own(e)
            basis[i, k - 1] = own(p)
            near = (xp, xm, yp, ym, VV[i, k + 1], VV[i, k - 1])
            t = seven(-cut(C[6, k - 1]), [cut(C[n, k - 1]) for n in range(6)], cut(p), [cut(a) for a in near])
            t = t + cut(C[7, k - 1]) * cut(ys(d, 1) - ys(d, -1))
            if last:
                T[k, 8:16] = t
            else:
                T[k] = t
            return carry

        lax.fori_loop(1, nz + 1, flat, 0, unroll=4)
        pairs = [(j, i + 1) for j in range(i + 2)]

        def deep(k, acc, i=i, cut=cut, last=last, pairs=pairs):
            v = cut(T[k]) + cut(C[8, k - 1]) * (cut(D[k + 1]) - cut(D[k - 1]))
            v = v + cut(C[9, k - 1]) * (cut(E[k + 1]) - cut(E[k - 1]))
            if not last:
                VV[i + 1, k] = v
                v = own(v)
            vs = [own(VV[j, k]) for j in range(i + 1)] + [v]
            return tuple(s + vs[j] * v for s, (j, _) in zip(acc, pairs))

        start = (jnp.zeros((8, 128), F32),) * len(pairs)
        acc = lax.fori_loop(1, nz + 1, deep, start, unroll=4)
        for s, key in zip(acc, pairs):
            sums[key] = s
    lane8 = lanes((8, 128))
    core_part = (lane8 >= 4) & (lane8 < 124)
    line = lanes((1, 128))
    out = jnp.zeros((1, 128), F32)
    for n, (i, j) in enumerate(KEYS):
        s = jnp.where(core_part, sums[(i, j)], 0.0) + rims[i] * rims[j]
        s = jnp.sum(jnp.sum(s, axis=0, keepdims=True), axis=1, keepdims=True)
        out = jnp.where(line == n, s, out)
    gram[...] = jnp.broadcast_to(out, gram.shape)


KEYS = ((0, 1), (1, 1), (0, 2), (1, 2), (2, 2), (0, 3), (1, 3), (2, 3), (3, 3))


def weights(gram):
    def inner(a, b):
        total = 0.0
        for i in range(4):
            for j in range(4):
                if a[i] is not None and b[j] is not None:
                    total = total + a[i] * b[j] * gram[(min(i, j), max(i, j))]
        return total

    def less(a, s, b):
        out = []
        for one, two in zip(a, b):
            if two is None:
                out.append(one)
            else:
                out.append(-(s * two) if one is None else one - s * two)
        return out

    one = jnp.ones((1, 1), F32)
    r = [one, None, None, None]
    sol = [None] * 4
    dirs, images, norms = [r], [[None, one, None, None]], []
    for n in range(ITERS):
        norms.append(inner(images[n], images[n]))
        beta = inner(r, images[n]) / norms[n]
        sol = less(sol, -beta, dirs[n])
        r = less(r, beta, images[n])
        if n + 1 < ITERS:
            z = [None] + r[:3]
            new_dir, new_img = r, z
            for l in range(n + 1):
                alpha = inner(z, images[l]) / norms[l]
                new_dir = less(new_dir, alpha, dirs[l])
                new_img = less(new_img, alpha, images[l])
            dirs.append(new_dir)
            images.append(new_img)
    return sol[:3]


def last_kernel(
    partial, moved, basis, dxs, dys, rim_moved, rim_basis, rim_dxs, rim_dys,
    momenta_out, theta_out, pressure,
):
    nz = moved.shape[1]
    total = jnp.sum(partial[...], axis=0, keepdims=True)
    line = lanes(total.shape)
    gram = {
        key: jnp.sum(jnp.where(line == n, total, 0.0), axis=1, keepdims=True)
        for n, key in enumerate(KEYS)
    }
    c = [jnp.broadcast_to(s, (8, 128)) for s in weights(gram)]
    h = [0.5 * s for s in c]
    lane = lanes((8, 128))

    def mix(s, a):
        return (s[0] * a[0] + s[1] * a[1]) + s[2] * a[2]

    def joined(rim, core):
        turned = [roll(rim, -8 * k, 1) for k in range(nz)]
        return [
            jnp.where(lane < 4, turned[k], jnp.where(lane >= 124, turned[(k + 1) % nz], core[k]))
            for k in range(nz)
        ]

    p_rim = mix(c, rim_basis)
    p = joined(p_rim, [mix(c, [basis[i, k] for i in range(3)]) for k in range(nz)])
    for k in range(nz):
        pressure[k] = p[k]
    zero = jnp.zeros((8, 128), F32)
    for n, (diff, rim_diff) in enumerate(((dxs, rim_dxs), (dys, rim_dys))):
        core = [moved[n, k] - mix(h, [diff[i, k] for i in range(3)]) for k in range(nz)]
        for k, a in enumerate(joined(rim_moved[n] - mix(h, rim_diff), core)):
            momenta_out[n, k] = a
    for k, a in enumerate(joined(rim_moved[2], [moved[2, k] for k in range(nz)])):
        above = p[k + 1] if k + 1 < nz else zero
        below = p[k - 1] if k > 0 else zero
        momenta_out[2, k] = a - 0.5 * (above - below)
    for k, a in enumerate(joined(rim_moved[3], [moved[3, k] for k in range(nz)])):
        theta_out[k] = a


def shift_to(a, axis, step):
    n = lax.axis_size(axis)
    return lax.ppermute(a, axis, [(i, (i + step) % n) for i in range(n)])


def call(kernel, name, out, scratch=(), space=pltpu.VMEM, limit=16):
    def run(*args):
        return pl.pallas_call(
            kernel,
            out_shape=tuple(jax.ShapeDtypeStruct(a, F32) for a in out),
            in_specs=[pl.BlockSpec(memory_space=space)] * len(args),
            out_specs=[pl.BlockSpec(memory_space=pltpu.VMEM)] * len(out),
            scratch_shapes=list(scratch),
            compiler_params=pltpu.CompilerParams(vmem_limit_bytes=limit << 20),
            name=name,
        )(*args)

    return run


def local(momenta, theta, courant, density, metric_diag, metric_cross):
    nz = density.shape[0]
    args = (momenta, theta, courant, density, metric_diag, metric_cross)
    block = (nz, 8, 128)
    core = (nz, 24, 128)
    deep = (nz + 2, 24, 128)
    nx, ny = lax.axis_size("gx"), lax.axis_size("gy")
    rows_out = (len(COMBOS), nz, 8, 128)

    *args, to_up, to_down = call(
        fetch_kernel,
        "fetch",
        [a.shape for a in args] + [rows_out] * 2,
        [pltpu.SemaphoreType.DMA((6,))],
        pltpu.HBM,
    )(*(pltpu.with_memory_space_constraint(a, pltpu.HBM) for a in args))
    below = shift_to(to_up, "gy", 1)
    above = shift_to(to_down, "gy", -1)
    S, to_left, to_right = call(
        strips_kernel, "strips", [(NF,) + deep] + [(NF, 24, 128)] * 2
    )(*args, below, above)
    from_left = shift_to(to_right, "gx", 1)
    from_right = shift_to(to_left, "gx", -1)
    moved, right_side, coef = call(
        core_kernel,
        "core",
        [(4,) + block, core, (10,) + core],
        [pltpu.VMEM((4,) + deep, F32), pltpu.VMEM((3,) + deep, F32)],
    )(S)
    three, rim = (3,) + block, (3, 8, 128)
    *parts, gram = call(
        solve_kernel,
        "solve",
        [three] * 3 + [(4, 8, 128), rim, rim, rim, (nx, 128)],
        [pltpu.VMEM((3,) + deep, F32)] + [pltpu.VMEM(deep, F32)] * 3,
    )(right_side, coef, to_left, to_right, from_left, from_right)

    part = lax.all_to_all(gram, "gx", 0, 0, tiled=True)
    part = jnp.broadcast_to(jnp.sum(part, axis=0, keepdims=True), (ny, 128))
    part = lax.all_to_all(part, "gy", 0, 0, tiled=True)
    momenta_out, theta_out, pressure = call(
        last_kernel, "combine", [three, block, block]
    )(part, moved, *parts)
    return (momenta_out, theta_out, pressure)


def solution(mesh):
    placed = (
        P(None, None, "gy", "gx"),
        P(None, "gy", "gx"),
        P(None, None, "gy", "gx"),
        P(None, "gy", "gx"),
        P(None, None, "gy", "gx"),
        P(None, None, "gy", "gx"),
    )
    return jax.shard_map(
        local,
        mesh=mesh,
        in_specs=placed,
        out_specs=(P(None, None, "gy", "gx"), P(None, "gy", "gx"), P(None, "gy", "gx")),
        check_vma=False,
    )
```

time: 80.9 us -> 78.5 us (0.970)
  starting transfers between devices: 25.8 us -> 20.4 us
  blocking collectives: 33.1 us -> 37.1 us
  Pallas kernels: 12.4 us -> 9.87 us
  waiting for transfers between devices: 8.36 us -> 10.1 us
    ppermute x6 -> x4, starting transfers between devices: 25.8 us -> 20.4 us  [shift_to(): return lax.ppermute(a, axis, [(i, (i + step) % n) for i in range(n)])]
    pallas_call x3 -> x5, Pallas kernels: 12.4 us -> 9.87 us  [run(): pl.pallas_call(kernel, out_shape=tuple((jax.ShapeDtypeStruct(a, F32) for...]
    all_to_all x1, blocking collectives: 18 us -> 20.2 us  [local(): part = lax.all_to_all(part, 'gy', 0, 0, tiled=True)]
    all_to_all x1, blocking collectives: 15.1 us -> 16.9 us  [local(): part = lax.all_to_all(gram, 'gx', 0, 0, tiled=True)]
    ppermute x6 -> x4, waiting for transfers between devices: 8.36 us -> 10.1 us  [shift_to(): return lax.ppermute(a, axis, [(i, (i + step) % n) for i in range(n)])]
  transfers between devices with their start and end apart: 6 -> 4, of which waited for: 2 -> 3; matrix products, arithmetic and copies ran while one was open for 0% -> 0% of each run, Pallas kernels for 0% -> 3%
where the time goes in v3:
time: 78.5 us; the launch traced here: 78.2 us
  blocking collectives  37.1 us (47%)
  starting transfers between devices  20.4 us (26%)
  waiting for transfers between devices  10.1 us (13%)
  Pallas kernels  9.87 us (13%)
    ppermute x4, starting transfers between devices, shift_to(): return lax.ppermute(a, axis, [(i, (i + step) % n) for i in range(n)])  20.4 us
    all_to_all x1, blocking collectives, local(): part = lax.all_to_all(part, 'gy', 0, 0, tiled=True)  20.2 us
    all_to_all x1, blocking collectives, local(): part = lax.all_to_all(gram, 'gx', 0, 0, tiled=True)  16.9 us
    ppermute x4, waiting for transfers between devices, shift_to(): return lax.ppermute(a, axis, [(i, (i + step) % n) for i in range(n)])  10.1 us
    pallas_call x5, Pallas kernels, run(): pl.pallas_call(kernel, out_shape=tuple((jax.ShapeDtypeStruct(a, F32) for...  9.87 us
  transfers between devices with their start and end apart: 4, of which 3 were waited for; matrix products, arithmetic and copies ran while one was open for 0% of the time, Pallas kernels for 3%

profile of v3, /device:TPU:1, one launch (start us, length us, event | category | flops | bytes accessed | tf_op | source)
XLA Modules:
  0.0 78.2 jit_solution(6038064278133425186)
XLA Ops:
  0.6 1.4 %fetch.1 = (f32[3,16,8,128]{3,2,1,0:T(8,128)S(1)}, f32[16,8,128]{2,1,0:T(8,128)S(1)}, f32[3,16,8,128]{3,2,1,0:T(8,128)S(1)}, f32[16,8,128]{2,1,0:T(8,128)S(1)}, ...) custom-call(f32[3,16,8,128]{3,2,1,0:T(8,128)} %refs_0_.1, ...), custom_call_target="tpu_custom_call" | custom-call | tf_op jit(solution)/shard_map/fetch/pallas_call | solution.py:463
  2.0 4.4 %collective-permute-start = (f32[7,16,8,128]{3,2,1,0:T(8,128)S(1)}, f32[7,16,8,128]{3,2,1,0:T(8,128)S(1)}, u32[]{:S(2)}, u32[]{:S(2)}) collective-permute-start(f32[7,16,8,128]{3,2,1,0:T(8,128)S(1)} %get-tuple-element.31), channel_id=1, source_target_pairs={{0,1},{1,2},{2,3},{3,4},{4,5},{5,6},{6,7},{7,8},{8,9},{9,10},{10,1... | collective-permute-start | bytes 1376264 | tf_op jit(solution)/shard_map/ppermute | solution.py:458
  6.4 9.5 %collective-permute-start.1 = (f32[7,16,8,128]{3,2,1,0:T(8,128)S(1)}, f32[7,16,8,128]{3,2,1,0:T(8,128)S(1)}, u32[]{:S(2)}, u32[]{:S(2)}) collective-permute-start(f32[7,16,8,128]{3,2,1,0:T(8,128)S(1)} %get-tuple-element.32), channel_id=1, source_target_pairs={{0,15},{1,0},{2,1},{3,2},{4,3},{5,4},{6,5},{7,6},{8,7},{9,8},{10,9... | collective-permute-start | bytes 1376264 | tf_op jit(solution)/shard_map/ppermute | solution.py:458
  15.9 8.3 %collective-permute-done.below = f32[7,16,8,128]{3,2,1,0:T(8,128)S(1)} collective-permute-done((f32[7,16,8,128]{3,2,1,0:T(8,128)S(1)}, f32[7,16,8,128]{3,2,1,0:T(8,128)S(1)}, u32[]{:S(2)}, u32[]{:S(2)}) %collective-permute-start) | collective-permute-done | bytes 458784 | tf_op jit(solution)/shard_map/ppermute | solution.py:458
  24.2 0.9 %collective-permute-done.1.above = f32[7,16,8,128]{3,2,1,0:T(8,128)S(1)} collective-permute-done((f32[7,16,8,128]{3,2,1,0:T(8,128)S(1)}, f32[7,16,8,128]{3,2,1,0:T(8,128)S(1)}, u32[]{:S(2)}, u32[]{:S(2)}) %collective-permute-start.1) | collective-permute-done | bytes 458784 | tf_op jit(solution)/shard_map/ppermute | solution.py:458
  25.1 1.6 %strips.1 = (f32[14,18,24,128]{3,2,1,0:T(8,128)S(1)}, f32[14,24,128]{2,1,0:T(8,128)S(1)}, f32[14,24,128]{2,1,0:T(8,128)S(1)}) custom-call(f32[3,16,8,128]{3,2,1,0:T(8,128)S(1)} %get-tuple-element.25.mom, f32[16,8,128]{2,1,0:T(8,128)S(1)} %get-tuple-element.26.th, f32[3,16,8,128]{3,2,1,0:T(8,128)S(1)} %get-tuple-element.27.cou, ...), custom_call_target="tpu_custom_call" | custom-call | tf_op jit(solution)/shard_map/strips/pallas_call | solution.py:463
  26.7 3.4 %collective-permute-start.3 = (f32[14,24,128]{2,1,0:T(8,128)S(1)}, f32[14,24,128]{2,1,0:T(8,128)S(1)}, u32[]{:S(2)}, u32[]{:S(2)}) collective-permute-start(f32[14,24,128]{2,1,0:T(8,128)S(1)} %get-tuple-element.36.to_left), channel_id=1, source_target_pairs={{0,496},{16,0},{32,16},{48,32},{64,48},{80,64},{96,80},{112,96},{1... | collective-permute-start | bytes 516104 | tf_op jit(solution)/shard_map/ppermute | solution.py:458
  30.1 3.1 %collective-permute-start.2 = (f32[14,24,128]{2,1,0:T(8,128)S(1)}, f32[14,24,128]{2,1,0:T(8,128)S(1)}, u32[]{:S(2)}, u32[]{:S(2)}) collective-permute-start(f32[14,24,128]{2,1,0:T(8,128)S(1)} %get-tuple-element.37.to_right), channel_id=1, source_target_pairs={{0,16},{16,32},{32,48},{48,64},{64,80},{80,96},{96,112},{112,128},... | collective-permute-start | bytes 516104 | tf_op jit(solution)/shard_map/ppermute | solution.py:458
  33.2 2.5 %core.1 = (f32[4,16,8,128]{3,2,1,0:T(8,128)S(1)}, f32[16,24,128]{2,1,0:T(8,128)S(1)}, f32[10,16,24,128]{3,2,1,0:T(8,128)S(1)}) custom-call(f32[14,18,24,128]{3,2,1,0:T(8,128)S(1)} %get-tuple-element.33.S), custom_call_target="tpu_custom_call" | custom-call | tf_op jit(solution)/shard_map/core/pallas_call | solution.py:463
  35.8 0.0 collective-permute-done.3.from_right
  35.8 0.9 %collective-permute-done.2.from_left = f32[14,24,128]{2,1,0:T(8,128)S(1)} collective-permute-done((f32[14,24,128]{2,1,0:T(8,128)S(1)}, f32[14,24,128]{2,1,0:T(8,128)S(1)}, u32[]{:S(2)}, u32[]{:S(2)}) %collective-permute-start.2) | collective-permute-done | bytes 172064 | tf_op jit(solution)/shard_map/ppermute | solution.py:458
  36.7 3.4 %solve.1 = (f32[3,16,8,128]{3,2,1,0:T(8,128)S(1)}, f32[3,16,8,128]{3,2,1,0:T(8,128)S(1)}, f32[3,16,8,128]{3,2,1,0:T(8,128)S(1)}, f32[4,8,128]{2,1,0:T(8,128)S(1)...) custom-call(f32[16,24,128]{2,1,0:T(8,128)S(1)} %get-tuple-element.34.r, ...), custom_call_target="tpu_custom_call" | custom-call | tf_op jit(solution)/shard_map/solve/pallas_call | solution.py:463
  40.1 16.9 %all_to_all.17 = f32[32,1,128]{2,1,0:T(1,128)S(1)} all-to-all(f32[32,1,128]{2,1,0:T(1,128)S(1)} %bitcast.5), channel_id=1, replica_groups=mesh['gx'=32,'gy'=16] {'gx'}, dimensions={0} | all-to-all | bytes 32768 | tf_op jit(solution)/shard_map/all_to_all | solution.py:513
  57.0 0.1 reduce_sum.9
  57.1 20.2 %all_to_all.18 = f32[16,1,128]{2,1,0:T(1,128)S(1)} all-to-all(f32[16,1,128]{2,1,0:T(1,128)S(1)} %broadcast_in_dim.2), channel_id=1, replica_groups=mesh['gx'=32,'gy'=16] {'gy'}, dimensions={0} | all-to-all | bytes 16384 | tf_op jit(solution)/shard_map/all_to_all | solution.py:515
  77.2 0.9 %combine.1 = (f32[3,16,8,128]{3,2,1,0:T(8,128)}, f32[16,8,128]{2,1,0:T(8,128)}, f32[16,8,128]{2,1,0:T(8,128)}) custom-call(f32[16,128]{1,0:T(8,128)S(1)} %bitcast.4, f32[4,16,8,128]{3,2,1,0:T(8,128)S(1)} %get-tuple-element.39.moved, f32[3,16,8,128]{3,2,1,0:T(8,128)S(1)} %get-tuple-element.40.basis, f32[3,16,8,128]{3,2,1,0:T(8,128)S(1)} %get-tuple-element.41.dxs, ...), custom_call_target="tpu_custom_call" | custom-call | tf_op jit(solution)/shard_map/combine/pallas_call | solution.py:463
  (1 shorter events, 0.0 us)
Async XLA Ops:
  2.0 22.2 %collective-permute-start = (f32[7,16,8,128]{3,2,1,0:T(8,128)S(1)}, f32[7,16,8,128]{3,2,1,0:T(8,128)S(1)}, u32[]{:S(2)}, u32[]{:S(2)}) collective-permute-start(f32[7,16,8,128]{3,2,1,0:T(8,128)S(1)} %get-tuple-element.31), channel_id=1, source_target_pairs={{0,1},{1,2},{2,3},{3,4},{4,5},{5,6},{6,7},{7,8},{8,9},{9,10},{10,1... | collective-permute-start | bytes 1376264 | tf_op jit(solution)/shard_map/ppermute | solution.py:458
  6.4 18.7 %collective-permute-start.1 = (f32[7,16,8,128]{3,2,1,0:T(8,128)S(1)}, f32[7,16,8,128]{3,2,1,0:T(8,128)S(1)}, u32[]{:S(2)}, u32[]{:S(2)}) collective-permute-start(f32[7,16,8,128]{3,2,1,0:T(8,128)S(1)} %get-tuple-element.32), channel_id=1, source_target_pairs={{0,15},{1,0},{2,1},{3,2},{4,3},{5,4},{6,5},{7,6},{8,7},{9,8},{10,9... | collective-permute-start | bytes 1376264 | tf_op jit(solution)/shard_map/ppermute | solution.py:458
  26.7 9.1 %collective-permute-start.3 = (f32[14,24,128]{2,1,0:T(8,128)S(1)}, f32[14,24,128]{2,1,0:T(8,128)S(1)}, u32[]{:S(2)}, u32[]{:S(2)}) collective-permute-start(f32[14,24,128]{2,1,0:T(8,128)S(1)} %get-tuple-element.36.to_left), channel_id=1, source_target_pairs={{0,496},{16,0},{32,16},{48,32},{64,48},{80,64},{96,80},{112,96},{1... | collective-permute-start | bytes 516104 | tf_op jit(solution)/shard_map/ppermute | solution.py:458
  30.1 6.6 %collective-permute-start.2 = (f32[14,24,128]{2,1,0:T(8,128)S(1)}, f32[14,24,128]{2,1,0:T(8,128)S(1)}, u32[]{:S(2)}, u32[]{:S(2)}) collective-permute-start(f32[14,24,128]{2,1,0:T(8,128)S(1)} %get-tuple-element.37.to_right), channel_id=1, source_target_pairs={{0,16},{16,32},{32,48},{48,64},{64,80},{80,96},{96,112},{112,128},... | collective-permute-start | bytes 516104 | tf_op jit(solution)/shard_map/ppermute | solution.py:458

commit v4 on v3

--- a/solution.py
+++ b/solution.py
@@ -106,8 +106,19 @@
     return cro.at[f - 11]
 
 
+def strips(levels):
+    nz = len(levels)
+    slot = lanes(levels[0].shape) // 8
+    left = right = jnp.zeros(levels[0].shape, F32)
+    for k, a in enumerate(levels):
+        moved = roll(a, 8 * k, 1)
+        left = jnp.where(slot == k, moved, left)
+        right = jnp.where(slot == (k - 1) % nz, moved, right)
+    return left, roll(right, 8, 1)
+
+
 def fetch_kernel(*refs):
-    sources, refs, (to_up, to_down, sem) = refs[:6], refs[6:12], refs[12:]
+    sources, refs, (to_chip, to_other, to_up, to_down, sem) = refs[:6], refs[6:12], refs[12:]
     copies = [pltpu.make_async_copy(a, b, sem.at[i]) for i, (a, b) in enumerate(zip(sources, refs))]
     for copy in copies:
         copy.start()
@@ -126,34 +137,37 @@
             a, b = one[k], two[k]
             to_down[c, k] = jnp.where(row < n, a, roll(b, n, 0))
             to_up[c, k] = jnp.where(row >= 8 - n, a, roll(b, -n, 0))
-
-
-def strips_kernel(mom, th, cou, den, dia, cro, below, above, S, to_left, to_right):
-    refs = (mom, th, cou, den, dia, cro)
-    nz = den.shape[0]
+    for f in range(NF):
+        ref = field_of(refs, f)
+        left, right = strips([ref[k] for k in range(nz)])
+        to_chip[f] = jnp.where(even_x(), right, left)
+        to_other[f] = jnp.where(even_x(), left, right)
+
+
+def even_x():
+    return lax.axis_index("gx") % 2 == 0
+
+
+def by_side(chip, other):
+    return jnp.where(even_x(), other, chip), jnp.where(even_x(), chip, other)
+
+
+def corner_kernel(from_chip, from_other, to_up, to_down):
+    row = rows((8, 128))
+    for side in range(2):
+        for c, (first, n, second, m) in enumerate(COMBOS):
+            a, b = (by_side(from_chip[f], from_other[f])[side] for f in (first, second))
+            to_down[side, c] = jnp.where(row < n, a, roll(b, n, 0))
+            to_up[side, c] = jnp.where(row >= 8 - n, a, roll(b, -n, 0))
+
+
+def halo(f, low, high):
     gy = lax.axis_index("gy")
-    has_below = gy > 0
-    has_above = gy < lax.axis_size("gy") - 1
-    slot = lanes((24, 128)) // 8
-    for c, (first, n, second, m) in enumerate(COMBOS):
-        for f, shift in ((first, 0), (second, n)):
-            ref = field_of(refs, f)
-            outside = 1.0 if f == G else 0.0
-            left = jnp.zeros((24, 128), F32)
-            right = jnp.zeros((24, 128), F32)
-            for k in range(nz):
-                low = jnp.where(has_below, roll(below[c, k], shift, 0), outside)
-                high = jnp.where(has_above, roll(above[c, k], -shift, 0), outside)
-                whole = jnp.concatenate((low, ref[k], high), axis=0)
-                S[f, k + 1] = whole
-                moved = roll(whole, 8 * k, 1)
-                left = jnp.where(slot == k, moved, left)
-                right = jnp.where(slot == (k - 1) % nz, moved, right)
-            to_left[f] = left
-            to_right[f] = roll(right, 8, 1)
-            pad = jnp.full((24, 128), outside, F32)
-            S[f, 0] = pad
-            S[f, nz + 1] = pad
+    outside = 1.0 if f == G else 0.0
+    return (
+        jnp.where(gy > 0, low, outside),
+        jnp.where(gy < lax.axis_size("gy") - 1, high, outside),
+    )
 
 
 def masks(shape):
@@ -166,9 +180,27 @@
     return inside, edge
 
 
-def core_kernel(S, moved, right_side, C, P1, M):
-    nz = moved.shape[1]
+def core_kernel(
+    mom, th, cou, den, dia, cro, to_chip, to_other, below, above,
+    moved, right_side, C, near_left, near_right, S, P1, M,
+):
+    refs = (mom, th, cou, den, dia, cro)
+    nz = den.shape[0]
     shape = (24, 128)
+    for c, (first, n, second, m) in enumerate(COMBOS):
+        for f, shift in ((first, 0), (second, n)):
+            ref = field_of(refs, f)
+            outer = []
+            for k in range(nz):
+                low, high = halo(f, roll(below[c, k], shift, 0), roll(above[c, k], -shift, 0))
+                S[f, k + 1] = jnp.concatenate((low, ref[k], high), axis=0)
+                outer.append(jnp.concatenate((low, high), axis=0))
+            own_strips = by_side(to_chip[f], to_other[f])
+            for out, mid, ends in zip((near_left, near_right), own_strips, strips(outer)):
+                out[f] = jnp.concatenate((ends[0:8], mid, ends[8:16]), axis=0)
+            pad = jnp.full(shape, 1.0 if f == G else 0.0, F32)
+            S[f, 0] = pad
+            S[f, nz + 1] = pad
     inside, edge = masks(shape)
     zero = jnp.zeros(shape, F32)
 
@@ -229,7 +261,7 @@
 
 
 def solve_kernel(
-    right_side, C, to_left, to_right, from_left, from_right,
+    right_side, C, near_left, near_right, from_chip, from_other, cbelow, cabove,
     basis, dxs, dys, rim_moved, rim_basis, rim_dxs, rim_dys, gram,
     VV, D, E, T,
 ):
@@ -239,8 +271,18 @@
     inside, edge = masks((96, 128))
     lane96 = lanes((96, 128))
 
+    far = {}
+    for c, (one, n, two, m) in enumerate(COMBOS):
+        for f, shift in ((one, 0), (two, n)):
+            far[f] = []
+            for side, mine in enumerate(by_side(from_chip[f], from_other[f])):
+                low, high = halo(
+                    f, roll(cbelow[side, c], shift, 0), roll(cabove[side, c], -shift, 0)
+                )
+                far[f].append(jnp.concatenate((low, mine, high), axis=0))
+
     def rim_field(f):
-        return jnp.concatenate((from_left[f], to_right[f], to_left[f], from_right[f]), axis=0)
+        return jnp.concatenate((far[f][0], near_right[f], near_left[f], far[f][1]), axis=0)
 
     def around(q):
         return (
@@ -458,7 +500,15 @@
     return lax.ppermute(a, axis, [(i, (i + step) % n) for i in range(n)])
 
 
-def call(kernel, name, out, scratch=(), space=pltpu.VMEM, limit=16):
+def swap(a, axis, start):
+    n = lax.axis_size(axis)
+    pairs = []
+    for i in range(start, n + start, 2):
+        pairs += [(i % n, (i + 1) % n), ((i + 1) % n, i % n)]
+    return lax.ppermute(a, axis, pairs)
+
+
+def call(kernel, name, out, scratch=(), space=pltpu.VMEM, limit=16, cost=None):
     def run(*args):
         return pl.pallas_call(
             kernel,
@@ -467,6 +517,7 @@
             out_specs=[pl.BlockSpec(memory_space=pltpu.VMEM)] * len(out),
             scratch_shapes=list(scratch),
             compiler_params=pltpu.CompilerParams(vmem_limit_bytes=limit << 20),
+            cost_estimate=cost,
             name=name,
         )(*args)
 
@@ -482,33 +533,39 @@
     nx, ny = lax.axis_size("gx"), lax.axis_size("gy")
     rows_out = (len(COMBOS), nz, 8, 128)
 
-    *args, to_up, to_down = call(
+    tiles = (NF, 8, 128)
+    *args, to_chip, to_other, to_up, to_down = call(
         fetch_kernel,
         "fetch",
-        [a.shape for a in args] + [rows_out] * 2,
+        [a.shape for a in args] + [tiles] * 2 + [rows_out] * 2,
         [pltpu.SemaphoreType.DMA((6,))],
         pltpu.HBM,
     )(*(pltpu.with_memory_space_constraint(a, pltpu.HBM) for a in args))
     below = shift_to(to_up, "gy", 1)
     above = shift_to(to_down, "gy", -1)
-    S, to_left, to_right = call(
-        strips_kernel, "strips", [(NF,) + deep] + [(NF, 24, 128)] * 2
-    )(*args, below, above)
-    from_left = shift_to(to_right, "gx", 1)
-    from_right = shift_to(to_left, "gx", -1)
-    moved, right_side, coef = call(
+    from_other = swap(to_other, "gx", 1)
+    from_chip = swap(to_chip, "gx", 0)
+    corner_up, corner_down = call(
+        corner_kernel,
+        "corner",
+        [(2, len(COMBOS), 8, 128)] * 2,
+        cost=pl.CostEstimate(flops=10**10, transcendentals=0, bytes_accessed=10**9),
+    )(from_chip, from_other)
+    cbelow = shift_to(corner_up, "gy", 1)
+    cabove = shift_to(corner_down, "gy", -1)
+    moved, right_side, coef, near_left, near_right = call(
         core_kernel,
         "core",
-        [(4,) + block, core, (10,) + core],
-        [pltpu.VMEM((4,) + deep, F32), pltpu.VMEM((3,) + deep, F32)],
-    )(S)
+        [(4,) + block, core, (10,) + core] + [(NF, 24, 128)] * 2,
+        [pltpu.VMEM((n,) + deep, F32) for n in (NF, 4, 3)],
+    )(*args, to_chip, to_other, below, above)
     three, rim = (3,) + block, (3, 8, 128)
     *parts, gram = call(
         solve_kernel,
         "solve",
         [three] * 3 + [(4, 8, 128), rim, rim, rim, (nx, 128)],
         [pltpu.VMEM((3,) + deep, F32)] + [pltpu.VMEM(deep, F32)] * 3,
-    )(right_side, coef, to_left, to_right, from_left, from_right)
+    )(right_side, coef, near_left, near_right, from_chip, from_other, cbelow, cabove)
 
     part = lax.all_to_all(gram, "gx", 0, 0, tiled=True)
     part = jnp.broadcast_to(jnp.sum(part, axis=0, keepdims=True), (ny, 128))

time: 78.5 us -> 75.9 us (0.967)
  waiting for transfers between devices: 10.1 us -> 0.02 us
  starting transfers between devices: 20.4 us -> 26.1 us
  blocking collectives: 37.1 us -> 38.4 us
    ppermute x0 -> x2, starting transfers between devices: none -> 10.7 us  [swap(): return lax.ppermute(a, axis, pairs)]
    ppermute x4, waiting for transfers between devices: 10.1 us -> 0.01 us  [shift_to(): return lax.ppermute(a, axis, [(i, (i + step) % n) for i in range(n)])]
    ppermute x4, starting transfers between devices: 20.4 us -> 15.3 us  [shift_to(): return lax.ppermute(a, axis, [(i, (i + step) % n) for i in range(n)])]
    all_to_all x1, blocking collectives: 16.9 us -> 17.8 us  [local(): part = lax.all_to_all(gram, 'gx', 0, 0, tiled=True)]
  transfers between devices with their start and end apart: 4 -> 6, of which waited for: 3 -> 0; matrix products, arithmetic and copies ran while one was open for 0% -> 0% of each run, Pallas kernels for 3% -> 5%
where the time goes in v4:
time: 75.9 us; the launch traced here: 75.6 us
  blocking collectives  38.4 us (51%)
  starting transfers between devices  26.1 us (34%)
  Pallas kernels  10.2 us (13%)
    all_to_all x1, blocking collectives, local(): part = lax.all_to_all(part, 'gy', 0, 0, tiled=True)  20.7 us
    all_to_all x1, blocking collectives, local(): part = lax.all_to_all(gram, 'gx', 0, 0, tiled=True)  17.8 us
    ppermute x4, starting transfers between devices, shift_to(): return lax.ppermute(a, axis, [(i, (i + step) % n) for i in range(n)])  15.3 us
    ppermute x2, starting transfers between devices, swap(): return lax.ppermute(a, axis, pairs)  10.7 us
    pallas_call x5, Pallas kernels, run(): pl.pallas_call(kernel, out_shape=tuple((jax.ShapeDtypeStruct(a, F32) for...  10.2 us
  transfers between devices with their start and end apart: 6, of which 0 were waited for; matrix products, arithmetic and copies ran while one was open for 0% of the time, Pallas kernels for 5%

profile of v4, /device:TPU:1, one launch (start us, length us, event | category | flops | bytes accessed | tf_op | source)
XLA Modules:
  0.0 75.6 jit_solution(1019110885228735855)
XLA Ops:
  0.6 2.1 %fetch.1 = (f32[3,16,8,128]{3,2,1,0:T(8,128)S(1)}, f32[16,8,128]{2,1,0:T(8,128)S(1)}, f32[3,16,8,128]{3,2,1,0:T(8,128)S(1)}, f32[16,8,128]{2,1,0:T(8,128)S(1)}, ...) custom-call(f32[3,16,8,128]{3,2,1,0:T(8,128)} %refs_0_.1, ...), custom_call_target="tpu_custom_call" | custom-call | tf_op jit(solution)/shard_map/fetch/pallas_call | solution.py:513
  2.7 8.8 %collective-permute-start.2 = (f32[14,8,128]{2,1,0:T(8,128)S(1)}, f32[14,8,128]{2,1,0:T(8,128)S(1)}, u32[]{:S(2)}, u32[]{:S(2)}) collective-permute-start(f32[14,8,128]{2,1,0:T(8,128)S(1)} %get-tuple-element.34.to_chip), channel_id=1, source_target_pairs={{0,16},{16,0},{32,48},{48,32},{64,80},{80,64},{96,112},{112,96},{1... | collective-permute-start | bytes 172040 | tf_op jit(solution)/shard_map/ppermute | solution.py:508
  11.5 1.9 %collective-permute-start.3 = (f32[14,8,128]{2,1,0:T(8,128)S(1)}, f32[14,8,128]{2,1,0:T(8,128)S(1)}, u32[]{:S(2)}, u32[]{:S(2)}) collective-permute-start(f32[14,8,128]{2,1,0:T(8,128)S(1)} %get-tuple-element.35.to_other), channel_id=1, source_target_pairs={{16,32},{32,16},{48,64},{64,48},{80,96},{96,80},{112,128},{128,112... | collective-permute-start | bytes 172040 | tf_op jit(solution)/shard_map/ppermute | solution.py:508
  13.4 1.9 %collective-permute-start = (f32[7,16,8,128]{3,2,1,0:T(8,128)S(1)}, f32[7,16,8,128]{3,2,1,0:T(8,128)S(1)}, u32[]{:S(2)}, u32[]{:S(2)}) collective-permute-start(f32[7,16,8,128]{3,2,1,0:T(8,128)S(1)} %get-tuple-element.36), channel_id=1, source_target_pairs={{0,1},{1,2},{2,3},{3,4},{4,5},{5,6},{6,7},{7,8},{8,9},{9,10},{10,1... | collective-permute-start | bytes 1376264 | tf_op jit(solution)/shard_map/ppermute | solution.py:500
  15.3 6.9 %collective-permute-start.1 = (f32[7,16,8,128]{3,2,1,0:T(8,128)S(1)}, f32[7,16,8,128]{3,2,1,0:T(8,128)S(1)}, u32[]{:S(2)}, u32[]{:S(2)}) collective-permute-start(f32[7,16,8,128]{3,2,1,0:T(8,128)S(1)} %get-tuple-element.37), channel_id=1, source_target_pairs={{0,15},{1,0},{2,1},{3,2},{4,3},{5,4},{6,5},{7,6},{8,7},{9,8},{10,9... | collective-permute-start | bytes 1376264 | tf_op jit(solution)/shard_map/ppermute | solution.py:500
  22.3 0.0 collective-permute-done.2.from_chip
  22.3 0.0 collective-permute-done.3.from_other
  22.3 1.9 %collective-permute-start.4 = (f32[2,7,8,128]{3,2,1,0:T(8,128)S(1)}, f32[2,7,8,128]{3,2,1,0:T(8,128)S(1)}, u32[]{:S(2)}, u32[]{:S(2)}) collective-permute-start(f32[2,7,8,128]{3,2,1,0:T(8,128)S(1)} %get-tuple-element.42), channel_id=1, source_target_pairs={{0,1},{1,2},{2,3},{3,4},{4,5},{5,6},{6,7},{7,8},{8,9},{9,10},{10,1... | collective-permute-start | bytes 172040 | tf_op jit(solution)/shard_map/ppermute | solution.py:500
  24.3 4.6 %collective-permute-start.5 = (f32[2,7,8,128]{3,2,1,0:T(8,128)S(1)}, f32[2,7,8,128]{3,2,1,0:T(8,128)S(1)}, u32[]{:S(2)}, u32[]{:S(2)}) collective-permute-start(f32[2,7,8,128]{3,2,1,0:T(8,128)S(1)} %get-tuple-element.43), channel_id=1, source_target_pairs={{0,15},{1,0},{2,1},{3,2},{4,3},{5,4},{6,5},{7,6},{8,7},{9,8},{10,9... | collective-permute-start | bytes 172040 | tf_op jit(solution)/shard_map/ppermute | solution.py:500
  28.8 0.0 collective-permute-done.below
  28.9 0.0 collective-permute-done.1.above
  28.9 3.8 %core.1 = (f32[4,16,8,128]{3,2,1,0:T(8,128)S(1)}, f32[16,24,128]{2,1,0:T(8,128)S(1)}, f32[10,16,24,128]{3,2,1,0:T(8,128)S(1)}, f32[14,24,128]{2,1,0:T(8,128)S(1)}, f32[14,24,128]{2,1,0:T(8,128)S(1)}) custom-call(f32[3,16,8,128]{3,2,1,0:T(8,128)S(1)} %get-tuple-element.28.mom, f32[16,8,128]{2,1,0:T(8,128)S(1)} %get-tuple-element.29.th, ...), custom_call_target="tpu_custom_call" | custom-call | tf_op jit(solution)/shard_map/core/pallas_call | solution.py:513
  32.7 0.0 collective-permute-done.4.cbelow
  32.7 0.0 collective-permute-done.5.cabove
  32.7 3.4 %solve.1 = (f32[3,16,8,128]{3,2,1,0:T(8,128)S(1)}, f32[3,16,8,128]{3,2,1,0:T(8,128)S(1)}, f32[3,16,8,128]{3,2,1,0:T(8,128)S(1)}, f32[4,8,128]{2,1,0:T(8,128)S(1)...) custom-call(f32[16,24,128]{2,1,0:T(8,128)S(1)} %get-tuple-element.38.r, ...), custom_call_target="tpu_custom_call" | custom-call | tf_op jit(solution)/shard_map/solve/pallas_call | solution.py:513
  36.1 17.8 %all_to_all.17 = f32[32,1,128]{2,1,0:T(1,128)S(1)} all-to-all(f32[32,1,128]{2,1,0:T(1,128)S(1)} %bitcast.5), channel_id=1, replica_groups=mesh['gx'=32,'gy'=16] {'gx'}, dimensions={0} | all-to-all | bytes 32768 | tf_op jit(solution)/shard_map/all_to_all | solution.py:570
  53.9 0.1 reduce_sum.9
  53.9 20.7 %all_to_all.18 = f32[16,1,128]{2,1,0:T(1,128)S(1)} all-to-all(f32[16,1,128]{2,1,0:T(1,128)S(1)} %broadcast_in_dim.2), channel_id=1, replica_groups=mesh['gx'=32,'gy'=16] {'gy'}, dimensions={0} | all-to-all | bytes 16384 | tf_op jit(solution)/shard_map/all_to_all | solution.py:572
  74.6 0.9 %combine.1 = (f32[3,16,8,128]{3,2,1,0:T(8,128)}, f32[16,8,128]{2,1,0:T(8,128)}, f32[16,8,128]{2,1,0:T(8,128)}) custom-call(f32[16,128]{1,0:T(8,128)S(1)} %bitcast.4, f32[4,16,8,128]{3,2,1,0:T(8,128)S(1)} %get-tuple-element.45.moved, f32[3,16,8,128]{3,2,1,0:T(8,128)S(1)} %get-tuple-element.46.basis, f32[3,16,8,128]{3,2,1,0:T(8,128)S(1)} %get-tuple-element.47.dxs, ...), custom_call_target="tpu_custom_call" | custom-call | tf_op jit(solution)/shard_map/combine/pallas_call | solution.py:513
  (2 shorter events, 0.0 us)
Async XLA Ops:
  2.7 19.6 %collective-permute-start.2 = (f32[14,8,128]{2,1,0:T(8,128)S(1)}, f32[14,8,128]{2,1,0:T(8,128)S(1)}, u32[]{:S(2)}, u32[]{:S(2)}) collective-permute-start(f32[14,8,128]{2,1,0:T(8,128)S(1)} %get-tuple-element.34.to_chip), channel_id=1, source_target_pairs={{0,16},{16,0},{32,48},{48,32},{64,80},{80,64},{96,112},{112,96},{1... | collective-permute-start | bytes 172040 | tf_op jit(solution)/shard_map/ppermute | solution.py:508
  11.5 10.8 %collective-permute-start.3 = (f32[14,8,128]{2,1,0:T(8,128)S(1)}, f32[14,8,128]{2,1,0:T(8,128)S(1)}, u32[]{:S(2)}, u32[]{:S(2)}) collective-permute-start(f32[14,8,128]{2,1,0:T(8,128)S(1)} %get-tuple-element.35.to_other), channel_id=1, source_target_pairs={{16,32},{32,16},{48,64},{64,48},{80,96},{96,80},{112,128},{128,112... | collective-permute-start | bytes 172040 | tf_op jit(solution)/shard_map/ppermute | solution.py:508
  13.4 15.4 %collective-permute-start = (f32[7,16,8,128]{3,2,1,0:T(8,128)S(1)}, f32[7,16,8,128]{3,2,1,0:T(8,128)S(1)}, u32[]{:S(2)}, u32[]{:S(2)}) collective-permute-start(f32[7,16,8,128]{3,2,1,0:T(8,128)S(1)} %get-tuple-element.36), channel_id=1, source_target_pairs={{0,1},{1,2},{2,3},{3,4},{4,5},{5,6},{6,7},{7,8},{8,9},{9,10},{10,1... | collective-permute-start | bytes 1376264 | tf_op jit(solution)/shard_map/ppermute | solution.py:500
  15.3 13.5 %collective-permute-start.1 = (f32[7,16,8,128]{3,2,1,0:T(8,128)S(1)}, f32[7,16,8,128]{3,2,1,0:T(8,128)S(1)}, u32[]{:S(2)}, u32[]{:S(2)}) collective-permute-start(f32[7,16,8,128]{3,2,1,0:T(8,128)S(1)} %get-tuple-element.37), channel_id=1, source_target_pairs={{0,15},{1,0},{2,1},{3,2},{4,3},{5,4},{6,5},{7,6},{8,7},{9,8},{10,9... | collective-permute-start | bytes 1376264 | tf_op jit(solution)/shard_map/ppermute | solution.py:500
  22.3 10.3 %collective-permute-start.4 = (f32[2,7,8,128]{3,2,1,0:T(8,128)S(1)}, f32[2,7,8,128]{3,2,1,0:T(8,128)S(1)}, u32[]{:S(2)}, u32[]{:S(2)}) collective-permute-start(f32[2,7,8,128]{3,2,1,0:T(8,128)S(1)} %get-tuple-element.42), channel_id=1, source_target_pairs={{0,1},{1,2},{2,3},{3,4},{4,5},{5,6},{6,7},{7,8},{8,9},{9,10},{10,1... | collective-permute-start | bytes 172040 | tf_op jit(solution)/shard_map/ppermute | solution.py:500
  24.3 8.4 %collective-permute-start.5 = (f32[2,7,8,128]{3,2,1,0:T(8,128)S(1)}, f32[2,7,8,128]{3,2,1,0:T(8,128)S(1)}, u32[]{:S(2)}, u32[]{:S(2)}) collective-permute-start(f32[2,7,8,128]{3,2,1,0:T(8,128)S(1)} %get-tuple-element.43), channel_id=1, source_target_pairs={{0,15},{1,0},{2,1},{3,2},{4,3},{5,4},{6,5},{7,6},{8,7},{9,8},{10,9... | collective-permute-start | bytes 172040 | tf_op jit(solution)/shard_map/ppermute | solution.py:500

commit v5 on v4

--- a/solution.py
+++ b/solution.py
@@ -152,13 +152,26 @@
     return jnp.where(even_x(), other, chip), jnp.where(even_x(), chip, other)
 
 
-def corner_kernel(from_chip, from_other, to_up, to_down):
+def corner_tiles(strip):
     row = rows((8, 128))
-    for side in range(2):
-        for c, (first, n, second, m) in enumerate(COMBOS):
-            a, b = (by_side(from_chip[f], from_other[f])[side] for f in (first, second))
-            to_down[side, c] = jnp.where(row < n, a, roll(b, n, 0))
-            to_up[side, c] = jnp.where(row >= 8 - n, a, roll(b, -n, 0))
+    for c, (first, n, second, m) in enumerate(COMBOS):
+        a, b = strip[first], strip[second]
+        up = jnp.where(row >= 8 - n, a, roll(b, -n, 0))
+        yield c, up, jnp.where(row < n, a, roll(b, n, 0))
+
+
+def other_kernel(from_other, to_up, to_down):
+    for c, up, down in corner_tiles(from_other):
+        to_up[c] = up
+        to_down[c] = down
+
+
+def chip_kernel(from_chip, other_up, other_down, to_up, to_down):
+    to_up[0] = other_up[...]
+    to_down[0] = other_down[...]
+    for c, up, down in corner_tiles(from_chip):
+        to_up[1, c] = up
+        to_down[1, c] = down
 
 
 def halo(f, low, high):
@@ -275,10 +288,10 @@
     for c, (one, n, two, m) in enumerate(COMBOS):
         for f, shift in ((one, 0), (two, n)):
             far[f] = []
+            lows = by_side(cbelow[1, c], cbelow[0, c])
+            highs = by_side(cabove[1, c], cabove[0, c])
             for side, mine in enumerate(by_side(from_chip[f], from_other[f])):
-                low, high = halo(
-                    f, roll(cbelow[side, c], shift, 0), roll(cabove[side, c], -shift, 0)
-                )
+                low, high = halo(f, roll(lows[side], shift, 0), roll(highs[side], -shift, 0))
                 far[f].append(jnp.concatenate((low, mine, high), axis=0))
 
     def rim_field(f):
@@ -545,12 +558,16 @@
     above = shift_to(to_down, "gy", -1)
     from_other = swap(to_other, "gx", 1)
     from_chip = swap(to_chip, "gx", 0)
-    corner_up, corner_down = call(
-        corner_kernel,
-        "corner",
-        [(2, len(COMBOS), 8, 128)] * 2,
+    pair = (len(COMBOS), 8, 128)
+    other_up, other_down = call(
+        other_kernel,
+        "other",
+        [pair] * 2,
         cost=pl.CostEstimate(flops=10**10, transcendentals=0, bytes_accessed=10**9),
-    )(from_chip, from_other)
+    )(from_other)
+    corner_up, corner_down = call(chip_kernel, "chip", [(2,) + pair] * 2)(
+        from_chip, other_up, other_down
+    )
     cbelow = shift_to(corner_up, "gy", 1)
     cabove = shift_to(corner_down, "gy", -1)
     moved, right_side, coef, near_left, near_right = call(

time: 75.9 us -> 73.4 us (0.967)
  blocking collectives: 38.4 us -> 31.4 us
  starting transfers between devices: 26.1 us -> 29.8 us
  waiting for transfers between devices: 0.02 us -> 0.86 us
    all_to_all x1, blocking collectives: 17.8 us -> 10.8 us  [local(): part = lax.all_to_all(gram, 'gx', 0, 0, tiled=True)]
    ppermute x4, starting transfers between devices: 15.3 us -> 19.5 us  [shift_to(): return lax.ppermute(a, axis, [(i, (i + step) % n) for i in range(n)])]
    ppermute x2, waiting for transfers between devices: 0.01 us -> 0.85 us  [swap(): return lax.ppermute(a, axis, pairs)]
    pallas_call x5 -> x6, Pallas kernels: 10.2 us -> 10.2 us  [run(): pl.pallas_call(kernel, out_shape=tuple((jax.ShapeDtypeStruct(a, F32) for...]
  transfers between devices with their start and end apart: 6 -> 6, of which waited for: 0 -> 1; matrix products, arithmetic and copies ran while one was open for 0% -> 0% of each run, Pallas kernels for 5% -> 5%
where the time goes in v5:
time: 73.4 us; the launch traced here: 73 us
  blocking collectives  31.4 us (43%)
  starting transfers between devices  29.8 us (41%)
  Pallas kernels  10.2 us (14%)
  waiting for transfers between devices  0.86 us (1%)
  between operations  0.75 us (1%)
    all_to_all x1, blocking collectives, local(): part = lax.all_to_all(part, 'gy', 0, 0, tiled=True)  20.5 us
    ppermute x4, starting transfers between devices, shift_to(): return lax.ppermute(a, axis, [(i, (i + step) % n) for i in range(n)])  19.5 us
    all_to_all x1, blocking collectives, local(): part = lax.all_to_all(gram, 'gx', 0, 0, tiled=True)  10.8 us
    ppermute x2, starting transfers between devices, swap(): return lax.ppermute(a, axis, pairs)  10.2 us
    pallas_call x6, Pallas kernels, run(): pl.pallas_call(kernel, out_shape=tuple((jax.ShapeDtypeStruct(a, F32) for...  10.2 us
  transfers between devices with their start and end apart: 6, of which 1 were waited for; matrix products, arithmetic and copies ran while one was open for 0% of the time, Pallas kernels for 5%

profile of v5, /device:TPU:1, one launch (start us, length us, event | category | flops | bytes accessed | tf_op | source)
XLA Modules:
  0.0 73.0 jit_solution(1589566156608703041)
XLA Ops:
  0.6 2.1 %fetch.1 = (f32[3,16,8,128]{3,2,1,0:T(8,128)S(1)}, f32[16,8,128]{2,1,0:T(8,128)S(1)}, f32[3,16,8,128]{3,2,1,0:T(8,128)S(1)}, f32[16,8,128]{2,1,0:T(8,128)S(1)}, ...) custom-call(f32[3,16,8,128]{3,2,1,0:T(8,128)} %refs_0_.1, ...), custom_call_target="tpu_custom_call" | custom-call | tf_op jit(solution)/shard_map/fetch/pallas_call | solution.py:526
  2.7 4.6 %collective-permute-start.3 = (f32[14,8,128]{2,1,0:T(8,128)S(1)}, f32[14,8,128]{2,1,0:T(8,128)S(1)}, u32[]{:S(2)}, u32[]{:S(2)}) collective-permute-start(f32[14,8,128]{2,1,0:T(8,128)S(1)} %get-tuple-element.37.to_other), channel_id=1, source_target_pairs={{16,32},{32,16},{48,64},{64,48},{80,96},{96,80},{112,128},{128,112... | collective-permute-start | bytes 172040 | tf_op jit(solution)/shard_map/ppermute | solution.py:521
  7.3 3.5 %collective-permute-start = (f32[7,16,8,128]{3,2,1,0:T(8,128)S(1)}, f32[7,16,8,128]{3,2,1,0:T(8,128)S(1)}, u32[]{:S(2)}, u32[]{:S(2)}) collective-permute-start(f32[7,16,8,128]{3,2,1,0:T(8,128)S(1)} %get-tuple-element.38), channel_id=1, source_target_pairs={{0,1},{1,2},{2,3},{3,4},{4,5},{5,6},{6,7},{7,8},{8,9},{9,10},{10,1... | collective-permute-start | bytes 1376264 | tf_op jit(solution)/shard_map/ppermute | solution.py:513
  10.8 9.5 %collective-permute-start.1 = (f32[7,16,8,128]{3,2,1,0:T(8,128)S(1)}, f32[7,16,8,128]{3,2,1,0:T(8,128)S(1)}, u32[]{:S(2)}, u32[]{:S(2)}) collective-permute-start(f32[7,16,8,128]{3,2,1,0:T(8,128)S(1)} %get-tuple-element.39), channel_id=1, source_target_pairs={{0,15},{1,0},{2,1},{3,2},{4,3},{5,4},{6,5},{7,6},{8,7},{9,8},{10,9... | collective-permute-start | bytes 1376264 | tf_op jit(solution)/shard_map/ppermute | solution.py:513
  20.4 5.7 %collective-permute-start.2 = (f32[14,8,128]{2,1,0:T(8,128)S(1)}, f32[14,8,128]{2,1,0:T(8,128)S(1)}, u32[]{:S(2)}, u32[]{:S(2)}) collective-permute-start(f32[14,8,128]{2,1,0:T(8,128)S(1)} %get-tuple-element.36.to_chip), channel_id=1, source_target_pairs={{0,16},{16,0},{32,48},{48,32},{64,80},{80,64},{96,112},{112,96},{1... | collective-permute-start | bytes 172040 | tf_op jit(solution)/shard_map/ppermute | solution.py:521
  26.0 0.0 collective-permute-done.3.from_other
  26.0 0.8 %collective-permute-done.2.from_chip = f32[14,8,128]{2,1,0:T(8,128)S(1)} collective-permute-done((f32[14,8,128]{2,1,0:T(8,128)S(1)}, f32[14,8,128]{2,1,0:T(8,128)S(1)}, u32[]{:S(2)}, u32[]{:S(2)}) %collective-permute-start.2) | collective-permute-done | bytes 57376 | tf_op jit(solution)/shard_map/ppermute | solution.py:521
  26.9 1.9 %collective-permute-start.4 = (f32[2,7,8,128]{3,2,1,0:T(8,128)S(1)}, f32[2,7,8,128]{3,2,1,0:T(8,128)S(1)}, u32[]{:S(2)}, u32[]{:S(2)}) collective-permute-start(f32[2,7,8,128]{3,2,1,0:T(8,128)S(1)} %get-tuple-element.46), channel_id=1, source_target_pairs={{0,1},{1,2},{2,3},{3,4},{4,5},{5,6},{6,7},{7,8},{8,9},{9,10},{10,1... | collective-permute-start | bytes 172040 | tf_op jit(solution)/shard_map/ppermute | solution.py:513
  28.8 4.6 %collective-permute-start.5 = (f32[2,7,8,128]{3,2,1,0:T(8,128)S(1)}, f32[2,7,8,128]{3,2,1,0:T(8,128)S(1)}, u32[]{:S(2)}, u32[]{:S(2)}) collective-permute-start(f32[2,7,8,128]{3,2,1,0:T(8,128)S(1)} %get-tuple-element.47), channel_id=1, source_target_pairs={{0,15},{1,0},{2,1},{3,2},{4,3},{5,4},{6,5},{7,6},{8,7},{9,8},{10,9... | collective-permute-start | bytes 172040 | tf_op jit(solution)/shard_map/ppermute | solution.py:513
  33.4 0.0 collective-permute-done.below
  33.4 0.0 collective-permute-done.1.above
  33.4 3.8 %core.1 = (f32[4,16,8,128]{3,2,1,0:T(8,128)S(1)}, f32[16,24,128]{2,1,0:T(8,128)S(1)}, f32[10,16,24,128]{3,2,1,0:T(8,128)S(1)}, f32[14,24,128]{2,1,0:T(8,128)S(1)}, f32[14,24,128]{2,1,0:T(8,128)S(1)}) custom-call(f32[3,16,8,128]{3,2,1,0:T(8,128)S(1)} %get-tuple-element.30.mom, f32[16,8,128]{2,1,0:T(8,128)S(1)} %get-tuple-element.31.th, ...), custom_call_target="tpu_custom_call" | custom-call | tf_op jit(solution)/shard_map/core/pallas_call | solution.py:526
  37.2 0.0 collective-permute-done.4.cbelow
  37.2 0.0 collective-permute-done.5.cabove
  37.2 3.4 %solve.1 = (f32[3,16,8,128]{3,2,1,0:T(8,128)S(1)}, f32[3,16,8,128]{3,2,1,0:T(8,128)S(1)}, f32[3,16,8,128]{3,2,1,0:T(8,128)S(1)}, f32[4,8,128]{2,1,0:T(8,128)S(1)...) custom-call(f32[16,24,128]{2,1,0:T(8,128)S(1)} %get-tuple-element.40.r, ...), custom_call_target="tpu_custom_call" | custom-call | tf_op jit(solution)/shard_map/solve/pallas_call | solution.py:526
  40.7 10.8 %all_to_all.17 = f32[32,1,128]{2,1,0:T(1,128)S(1)} all-to-all(f32[32,1,128]{2,1,0:T(1,128)S(1)} %bitcast.5), channel_id=1, replica_groups=mesh['gx'=32,'gy'=16] {'gx'}, dimensions={0} | all-to-all | bytes 32768 | tf_op jit(solution)/shard_map/all_to_all | solution.py:587
  51.5 0.1 reduce_sum.9
  51.6 20.5 %all_to_all.18 = f32[16,1,128]{2,1,0:T(1,128)S(1)} all-to-all(f32[16,1,128]{2,1,0:T(1,128)S(1)} %broadcast_in_dim.2), channel_id=1, replica_groups=mesh['gx'=32,'gy'=16] {'gy'}, dimensions={0} | all-to-all | bytes 16384 | tf_op jit(solution)/shard_map/all_to_all | solution.py:589
  72.1 0.9 %combine.1 = (f32[3,16,8,128]{3,2,1,0:T(8,128)}, f32[16,8,128]{2,1,0:T(8,128)}, f32[16,8,128]{2,1,0:T(8,128)}) custom-call(f32[16,128]{1,0:T(8,128)S(1)} %bitcast.4, f32[4,16,8,128]{3,2,1,0:T(8,128)S(1)} %get-tuple-element.49.moved, f32[3,16,8,128]{3,2,1,0:T(8,128)S(1)} %get-tuple-element.50.basis, f32[3,16,8,128]{3,2,1,0:T(8,128)S(1)} %get-tuple-element.51.dxs, ...), custom_call_target="tpu_custom_call" | custom-call | tf_op jit(solution)/shard_map/combine/pallas_call | solution.py:526
  (3 shorter events, 0.0 us)
Async XLA Ops:
  2.7 23.3 %collective-permute-start.3 = (f32[14,8,128]{2,1,0:T(8,128)S(1)}, f32[14,8,128]{2,1,0:T(8,128)S(1)}, u32[]{:S(2)}, u32[]{:S(2)}) collective-permute-start(f32[14,8,128]{2,1,0:T(8,128)S(1)} %get-tuple-element.37.to_other), channel_id=1, source_target_pairs={{16,32},{32,16},{48,64},{64,48},{80,96},{96,80},{112,128},{128,112... | collective-permute-start | bytes 172040 | tf_op jit(solution)/shard_map/ppermute | solution.py:521
  7.3 26.1 %collective-permute-start = (f32[7,16,8,128]{3,2,1,0:T(8,128)S(1)}, f32[7,16,8,128]{3,2,1,0:T(8,128)S(1)}, u32[]{:S(2)}, u32[]{:S(2)}) collective-permute-start(f32[7,16,8,128]{3,2,1,0:T(8,128)S(1)} %get-tuple-element.38), channel_id=1, source_target_pairs={{0,1},{1,2},{2,3},{3,4},{4,5},{5,6},{6,7},{7,8},{8,9},{9,10},{10,1... | collective-permute-start | bytes 1376264 | tf_op jit(solution)/shard_map/ppermute | solution.py:513
  10.8 22.6 %collective-permute-start.1 = (f32[7,16,8,128]{3,2,1,0:T(8,128)S(1)}, f32[7,16,8,128]{3,2,1,0:T(8,128)S(1)}, u32[]{:S(2)}, u32[]{:S(2)}) collective-permute-start(f32[7,16,8,128]{3,2,1,0:T(8,128)S(1)} %get-tuple-element.39), channel_id=1, source_target_pairs={{0,15},{1,0},{2,1},{3,2},{4,3},{5,4},{6,5},{7,6},{8,7},{9,8},{10,9... | collective-permute-start | bytes 1376264 | tf_op jit(solution)/shard_map/ppermute | solution.py:513
  20.4 6.5 %collective-permute-start.2 = (f32[14,8,128]{2,1,0:T(8,128)S(1)}, f32[14,8,128]{2,1,0:T(8,128)S(1)}, u32[]{:S(2)}, u32[]{:S(2)}) collective-permute-start(f32[14,8,128]{2,1,0:T(8,128)S(1)} %get-tuple-element.36.to_chip), channel_id=1, source_target_pairs={{0,16},{16,0},{32,48},{48,32},{64,80},{80,64},{96,112},{112,96},{1... | collective-permute-start | bytes 172040 | tf_op jit(solution)/shard_map/ppermute | solution.py:521
  26.9 10.3 %collective-permute-start.4 = (f32[2,7,8,128]{3,2,1,0:T(8,128)S(1)}, f32[2,7,8,128]{3,2,1,0:T(8,128)S(1)}, u32[]{:S(2)}, u32[]{:S(2)}) collective-permute-start(f32[2,7,8,128]{3,2,1,0:T(8,128)S(1)} %get-tuple-element.46), channel_id=1, source_target_pairs={{0,1},{1,2},{2,3},{3,4},{4,5},{5,6},{6,7},{7,8},{8,9},{9,10},{10,1... | collective-permute-start | bytes 172040 | tf_op jit(solution)/shard_map/ppermute | solution.py:513
  28.8 8.4 %collective-permute-start.5 = (f32[2,7,8,128]{3,2,1,0:T(8,128)S(1)}, f32[2,7,8,128]{3,2,1,0:T(8,128)S(1)}, u32[]{:S(2)}, u32[]{:S(2)}) collective-permute-start(f32[2,7,8,128]{3,2,1,0:T(8,128)S(1)} %get-tuple-element.47), channel_id=1, source_target_pairs={{0,15},{1,0},{2,1},{3,2},{4,3},{5,4},{6,5},{7,6},{8,7},{9,8},{10,9... | collective-permute-start | bytes 172040 | tf_op jit(solution)/shard_map/ppermute | solution.py:513

commit v6 on v5

--- a/solution.py
+++ b/solution.py
@@ -226,7 +226,7 @@
             P1[f, k] = seven(mid, w, psi, around)
         return carry
 
-    lax.fori_loop(1, nz + 1, upwind, 0, unroll=4)
+    lax.fori_loop(1, nz + 1, upwind, 0, unroll=8)
     for f in range(4):
         P1[f, 0] = zero
         P1[f, nz + 1] = zero
@@ -246,7 +246,7 @@
             moved[f, k - 1] = res[8:16]
         return ka
 
-    lax.fori_loop(1, nz + 1, anti, zero, unroll=4)
+    lax.fori_loop(1, nz + 1, anti, zero, unroll=8)
     M[2, 0] = zero
     M[2, nz + 1] = zero
 
@@ -270,7 +270,7 @@
         C[9, k - 1] = 0.25 * S[A23, k]
         return carry
 
-    lax.fori_loop(1, nz + 1, first, 0, unroll=4)
+    lax.fori_loop(1, nz + 1, first, 0, unroll=8)
 
 
 def solve_kernel(
@@ -397,7 +397,7 @@
                 T[k] = t
             return carry
 
-        lax.fori_loop(1, nz + 1, flat, 0, unroll=4)
+        lax.fori_loop(1, nz + 1, flat, 0, unroll=8)
         pairs = [(j, i + 1) for j in range(i + 2)]
 
         def deep(k, acc, i=i, cut=cut, last=last, pairs=pairs):
@@ -410,7 +410,7 @@
             return tuple(s + vs[j] * v for s, (j, _) in zip(acc, pairs))
 
         start = (jnp.zeros((8, 128), F32),) * len(pairs)
-        acc = lax.fori_loop(1, nz + 1, deep, start, unroll=4)
+        acc = lax.fori_loop(1, nz + 1, deep, start, unroll=8)
         for s, key in zip(acc, pairs):
             sums[key] = s
     lane8 = lanes((8, 128))

time: 73.4 us -> 72.9 us (level)
  no operation moved by 1% of the time
where the time goes in v6:
time: 72.9 us; the launch traced here: 72.5 us
  blocking collectives  31.4 us (43%)
  starting transfers between devices  29.8 us (41%)
  Pallas kernels  9.73 us (13%)
  waiting for transfers between devices  0.86 us (1%)
  between operations  0.75 us (1%)
    all_to_all x1, blocking collectives, local(): part = lax.all_to_all(part, 'gy', 0, 0, tiled=True)  20.5 us
    ppermute x4, starting transfers between devices, shift_to(): return lax.ppermute(a, axis, [(i, (i + step) % n) for i in range(n)])  19.5 us
    all_to_all x1, blocking collectives, local(): part = lax.all_to_all(gram, 'gx', 0, 0, tiled=True)  10.8 us
    ppermute x2, starting transfers between devices, swap(): return lax.ppermute(a, axis, pairs)  10.2 us
    pallas_call x6, Pallas kernels, run(): pl.pallas_call(kernel, out_shape=tuple((jax.ShapeDtypeStruct(a, F32) for...  9.73 us
  transfers between devices with their start and end apart: 6, of which 1 were waited for; matrix products, arithmetic and copies ran while one was open for 0% of the time, Pallas kernels for 5%

profile of v6, /device:TPU:1, one launch (start us, length us, event | category | flops | bytes accessed | tf_op | source)
XLA Modules:
  0.0 72.5 jit_solution(12896829772513567857)
XLA Ops:
  0.6 2.1 %fetch.1 = (f32[3,16,8,128]{3,2,1,0:T(8,128)S(1)}, f32[16,8,128]{2,1,0:T(8,128)S(1)}, f32[3,16,8,128]{3,2,1,0:T(8,128)S(1)}, f32[16,8,128]{2,1,0:T(8,128)S(1)}, ...) custom-call(f32[3,16,8,128]{3,2,1,0:T(8,128)} %refs_0_.1, ...), custom_call_target="tpu_custom_call" | custom-call | tf_op jit(solution)/shard_map/fetch/pallas_call | solution.py:526
  2.7 4.6 %collective-permute-start.3 = (f32[14,8,128]{2,1,0:T(8,128)S(1)}, f32[14,8,128]{2,1,0:T(8,128)S(1)}, u32[]{:S(2)}, u32[]{:S(2)}) collective-permute-start(f32[14,8,128]{2,1,0:T(8,128)S(1)} %get-tuple-element.37.to_other), channel_id=1, source_target_pairs={{16,32},{32,16},{48,64},{64,48},{80,96},{96,80},{112,128},{128,112... | collective-permute-start | bytes 172040 | tf_op jit(solution)/shard_map/ppermute | solution.py:521
  7.3 3.5 %collective-permute-start = (f32[7,16,8,128]{3,2,1,0:T(8,128)S(1)}, f32[7,16,8,128]{3,2,1,0:T(8,128)S(1)}, u32[]{:S(2)}, u32[]{:S(2)}) collective-permute-start(f32[7,16,8,128]{3,2,1,0:T(8,128)S(1)} %get-tuple-element.38), channel_id=1, source_target_pairs={{0,1},{1,2},{2,3},{3,4},{4,5},{5,6},{6,7},{7,8},{8,9},{9,10},{10,1... | collective-permute-start | bytes 1376264 | tf_op jit(solution)/shard_map/ppermute | solution.py:513
  10.8 9.5 %collective-permute-start.1 = (f32[7,16,8,128]{3,2,1,0:T(8,128)S(1)}, f32[7,16,8,128]{3,2,1,0:T(8,128)S(1)}, u32[]{:S(2)}, u32[]{:S(2)}) collective-permute-start(f32[7,16,8,128]{3,2,1,0:T(8,128)S(1)} %get-tuple-element.39), channel_id=1, source_target_pairs={{0,15},{1,0},{2,1},{3,2},{4,3},{5,4},{6,5},{7,6},{8,7},{9,8},{10,9... | collective-permute-start | bytes 1376264 | tf_op jit(solution)/shard_map/ppermute | solution.py:513
  20.4 5.7 %collective-permute-start.2 = (f32[14,8,128]{2,1,0:T(8,128)S(1)}, f32[14,8,128]{2,1,0:T(8,128)S(1)}, u32[]{:S(2)}, u32[]{:S(2)}) collective-permute-start(f32[14,8,128]{2,1,0:T(8,128)S(1)} %get-tuple-element.36.to_chip), channel_id=1, source_target_pairs={{0,16},{16,0},{32,48},{48,32},{64,80},{80,64},{96,112},{112,96},{1... | collective-permute-start | bytes 172040 | tf_op jit(solution)/shard_map/ppermute | solution.py:521
  26.0 0.0 collective-permute-done.3.from_other
  26.0 0.8 %collective-permute-done.2.from_chip = f32[14,8,128]{2,1,0:T(8,128)S(1)} collective-permute-done((f32[14,8,128]{2,1,0:T(8,128)S(1)}, f32[14,8,128]{2,1,0:T(8,128)S(1)}, u32[]{:S(2)}, u32[]{:S(2)}) %collective-permute-start.2) | collective-permute-done | bytes 57376 | tf_op jit(solution)/shard_map/ppermute | solution.py:521
  26.9 1.9 %collective-permute-start.4 = (f32[2,7,8,128]{3,2,1,0:T(8,128)S(1)}, f32[2,7,8,128]{3,2,1,0:T(8,128)S(1)}, u32[]{:S(2)}, u32[]{:S(2)}) collective-permute-start(f32[2,7,8,128]{3,2,1,0:T(8,128)S(1)} %get-tuple-element.46), channel_id=1, source_target_pairs={{0,1},{1,2},{2,3},{3,4},{4,5},{5,6},{6,7},{7,8},{8,9},{9,10},{10,1... | collective-permute-start | bytes 172040 | tf_op jit(solution)/shard_map/ppermute | solution.py:513
  28.8 4.6 %collective-permute-start.5 = (f32[2,7,8,128]{3,2,1,0:T(8,128)S(1)}, f32[2,7,8,128]{3,2,1,0:T(8,128)S(1)}, u32[]{:S(2)}, u32[]{:S(2)}) collective-permute-start(f32[2,7,8,128]{3,2,1,0:T(8,128)S(1)} %get-tuple-element.47), channel_id=1, source_target_pairs={{0,15},{1,0},{2,1},{3,2},{4,3},{5,4},{6,5},{7,6},{8,7},{9,8},{10,9... | collective-permute-start | bytes 172040 | tf_op jit(solution)/shard_map/ppermute | solution.py:513
  33.4 0.0 collective-permute-done.below
  33.4 0.0 collective-permute-done.1.above
  33.4 3.7 %core.1 = (f32[4,16,8,128]{3,2,1,0:T(8,128)S(1)}, f32[16,24,128]{2,1,0:T(8,128)S(1)}, f32[10,16,24,128]{3,2,1,0:T(8,128)S(1)}, f32[14,24,128]{2,1,0:T(8,128)S(1)}, f32[14,24,128]{2,1,0:T(8,128)S(1)}) custom-call(f32[3,16,8,128]{3,2,1,0:T(8,128)S(1)} %get-tuple-element.30.mom, f32[16,8,128]{2,1,0:T(8,128)S(1)} %get-tuple-element.31.th, ...), custom_call_target="tpu_custom_call" | custom-call | tf_op jit(solution)/shard_map/core/pallas_call | solution.py:526
  37.1 0.0 collective-permute-done.4.cbelow
  37.1 0.0 collective-permute-done.5.cabove
  37.2 3.0 %solve.1 = (f32[3,16,8,128]{3,2,1,0:T(8,128)S(1)}, f32[3,16,8,128]{3,2,1,0:T(8,128)S(1)}, f32[3,16,8,128]{3,2,1,0:T(8,128)S(1)}, f32[4,8,128]{2,1,0:T(8,128)S(1)...) custom-call(f32[16,24,128]{2,1,0:T(8,128)S(1)} %get-tuple-element.40.r, ...), custom_call_target="tpu_custom_call" | custom-call | tf_op jit(solution)/shard_map/solve/pallas_call | solution.py:526
  40.2 10.8 %all_to_all.17 = f32[32,1,128]{2,1,0:T(1,128)S(1)} all-to-all(f32[32,1,128]{2,1,0:T(1,128)S(1)} %bitcast.5), channel_id=1, replica_groups=mesh['gx'=32,'gy'=16] {'gx'}, dimensions={0} | all-to-all | bytes 32768 | tf_op jit(solution)/shard_map/all_to_all | solution.py:587
  51.0 0.1 reduce_sum.9
  51.1 20.5 %all_to_all.18 = f32[16,1,128]{2,1,0:T(1,128)S(1)} all-to-all(f32[16,1,128]{2,1,0:T(1,128)S(1)} %broadcast_in_dim.2), channel_id=1, replica_groups=mesh['gx'=32,'gy'=16] {'gy'}, dimensions={0} | all-to-all | bytes 16384 | tf_op jit(solution)/shard_map/all_to_all | solution.py:589
  71.6 0.9 %combine.1 = (f32[3,16,8,128]{3,2,1,0:T(8,128)}, f32[16,8,128]{2,1,0:T(8,128)}, f32[16,8,128]{2,1,0:T(8,128)}) custom-call(f32[16,128]{1,0:T(8,128)S(1)} %bitcast.4, f32[4,16,8,128]{3,2,1,0:T(8,128)S(1)} %get-tuple-element.49.moved, f32[3,16,8,128]{3,2,1,0:T(8,128)S(1)} %get-tuple-element.50.basis, f32[3,16,8,128]{3,2,1,0:T(8,128)S(1)} %get-tuple-element.51.dxs, ...), custom_call_target="tpu_custom_call" | custom-call | tf_op jit(solution)/shard_map/combine/pallas_call | solution.py:526
  (3 shorter events, 0.0 us)
Async XLA Ops:
  2.7 23.3 %collective-permute-start.3 = (f32[14,8,128]{2,1,0:T(8,128)S(1)}, f32[14,8,128]{2,1,0:T(8,128)S(1)}, u32[]{:S(2)}, u32[]{:S(2)}) collective-permute-start(f32[14,8,128]{2,1,0:T(8,128)S(1)} %get-tuple-element.37.to_other), channel_id=1, source_target_pairs={{16,32},{32,16},{48,64},{64,48},{80,96},{96,80},{112,128},{128,112... | collective-permute-start | bytes 172040 | tf_op jit(solution)/shard_map/ppermute | solution.py:521
  7.3 26.1 %collective-permute-start = (f32[7,16,8,128]{3,2,1,0:T(8,128)S(1)}, f32[7,16,8,128]{3,2,1,0:T(8,128)S(1)}, u32[]{:S(2)}, u32[]{:S(2)}) collective-permute-start(f32[7,16,8,128]{3,2,1,0:T(8,128)S(1)} %get-tuple-element.38), channel_id=1, source_target_pairs={{0,1},{1,2},{2,3},{3,4},{4,5},{5,6},{6,7},{7,8},{8,9},{9,10},{10,1... | collective-permute-start | bytes 1376264 | tf_op jit(solution)/shard_map/ppermute | solution.py:513
  10.8 22.6 %collective-permute-start.1 = (f32[7,16,8,128]{3,2,1,0:T(8,128)S(1)}, f32[7,16,8,128]{3,2,1,0:T(8,128)S(1)}, u32[]{:S(2)}, u32[]{:S(2)}) collective-permute-start(f32[7,16,8,128]{3,2,1,0:T(8,128)S(1)} %get-tuple-element.39), channel_id=1, source_target_pairs={{0,15},{1,0},{2,1},{3,2},{4,3},{5,4},{6,5},{7,6},{8,7},{9,8},{10,9... | collective-permute-start | bytes 1376264 | tf_op jit(solution)/shard_map/ppermute | solution.py:513
  20.4 6.5 %collective-permute-start.2 = (f32[14,8,128]{2,1,0:T(8,128)S(1)}, f32[14,8,128]{2,1,0:T(8,128)S(1)}, u32[]{:S(2)}, u32[]{:S(2)}) collective-permute-start(f32[14,8,128]{2,1,0:T(8,128)S(1)} %get-tuple-element.36.to_chip), channel_id=1, source_target_pairs={{0,16},{16,0},{32,48},{48,32},{64,80},{80,64},{96,112},{112,96},{1... | collective-permute-start | bytes 172040 | tf_op jit(solution)/shard_map/ppermute | solution.py:521
  26.9 10.2 %collective-permute-start.4 = (f32[2,7,8,128]{3,2,1,0:T(8,128)S(1)}, f32[2,7,8,128]{3,2,1,0:T(8,128)S(1)}, u32[]{:S(2)}, u32[]{:S(2)}) collective-permute-start(f32[2,7,8,128]{3,2,1,0:T(8,128)S(1)} %get-tuple-element.46), channel_id=1, source_target_pairs={{0,1},{1,2},{2,3},{3,4},{4,5},{5,6},{6,7},{7,8},{8,9},{9,10},{10,1... | collective-permute-start | bytes 172040 | tf_op jit(solution)/shard_map/ppermute | solution.py:513
  28.8 8.3 %collective-permute-start.5 = (f32[2,7,8,128]{3,2,1,0:T(8,128)S(1)}, f32[2,7,8,128]{3,2,1,0:T(8,128)S(1)}, u32[]{:S(2)}, u32[]{:S(2)}) collective-permute-start(f32[2,7,8,128]{3,2,1,0:T(8,128)S(1)} %get-tuple-element.47), channel_id=1, source_target_pairs={{0,15},{1,0},{2,1},{3,2},{4,3},{5,4},{6,5},{7,6},{8,7},{9,8},{10,9... | collective-permute-start | bytes 172040 | tf_op jit(solution)/shard_map/ppermute | solution.py:513

commit v7 on v6

--- a/solution.py
+++ b/solution.py
@@ -122,26 +122,27 @@
     copies = [pltpu.make_async_copy(a, b, sem.at[i]) for i, (a, b) in enumerate(zip(sources, refs))]
     for copy in copies:
         copy.start()
-    for copy in copies:
-        copy.wait()
     cou = refs[2]
     nz = refs[1].shape[0]
     row = rows((8, 128))
     first_row = (row == 0) & (lax.axis_index("gy") == 0)
-    for k in range(nz):
-        cou[1, k] = jnp.where(first_row, 0.0, cou[1, k])
-    cou[2, 0] = jnp.zeros((8, 128), F32)
+    for i, fields in enumerate(((U, V, W), (TH,), (CX, CY, CZ), (G,), (A11, A22, A33), (A12, A13, A23))):
+        copies[i].wait()
+        if i == 2:
+            for k in range(nz):
+                cou[1, k] = jnp.where(first_row, 0.0, cou[1, k])
+            cou[2, 0] = jnp.zeros((8, 128), F32)
+        for f in fields:
+            ref = field_of(refs, f)
+            left, right = strips([ref[k] for k in range(nz)])
+            to_chip[f] = jnp.where(even_x(), right, left)
+            to_other[f] = jnp.where(even_x(), left, right)
     for c, (first, n, second, m) in enumerate(COMBOS):
         one, two = field_of(refs, first), field_of(refs, second)
         for k in range(nz):
             a, b = one[k], two[k]
             to_down[c, k] = jnp.where(row < n, a, roll(b, n, 0))
             to_up[c, k] = jnp.where(row >= 8 - n, a, roll(b, -n, 0))
-    for f in range(NF):
-        ref = field_of(refs, f)
-        left, right = strips([ref[k] for k in range(nz)])
-        to_chip[f] = jnp.where(even_x(), right, left)
-        to_other[f] = jnp.where(even_x(), left, right)
 
 
 def even_x():

time: 72.9 us -> 72.9 us (level)
  no operation moved by 1% of the time
where the time goes in v7:
time: 72.9 us; the launch traced here: 72.6 us
  blocking collectives  31.4 us (43%)
  starting transfers between devices  29.8 us (41%)
  Pallas kernels  9.76 us (13%)
  waiting for transfers between devices  0.86 us (1%)
  between operations  0.75 us (1%)
    all_to_all x1, blocking collectives, local(): part = lax.all_to_all(part, 'gy', 0, 0, tiled=True)  20.5 us
    ppermute x4, starting transfers between devices, shift_to(): return lax.ppermute(a, axis, [(i, (i + step) % n) for i in range(n)])  19.5 us
    all_to_all x1, blocking collectives, local(): part = lax.all_to_all(gram, 'gx', 0, 0, tiled=True)  10.8 us
    ppermute x2, starting transfers between devices, swap(): return lax.ppermute(a, axis, pairs)  10.2 us
    pallas_call x6, Pallas kernels, run(): pl.pallas_call(kernel, out_shape=tuple((jax.ShapeDtypeStruct(a, F32) for...  9.76 us
  transfers between devices with their start and end apart: 6, of which 1 were waited for; matrix products, arithmetic and copies ran while one was open for 0% of the time, Pallas kernels for 5%

profile of v7, /device:TPU:1, one launch (start us, length us, event | category | flops | bytes accessed | tf_op | source)
XLA Modules:
  0.0 72.6 jit_solution(1955320265088928948)
XLA Ops:
  0.6 2.1 %fetch.1 = (f32[3,16,8,128]{3,2,1,0:T(8,128)S(1)}, f32[16,8,128]{2,1,0:T(8,128)S(1)}, f32[3,16,8,128]{3,2,1,0:T(8,128)S(1)}, f32[16,8,128]{2,1,0:T(8,128)S(1)}, ...) custom-call(f32[3,16,8,128]{3,2,1,0:T(8,128)} %refs_0_.1, ...), custom_call_target="tpu_custom_call" | custom-call | tf_op jit(solution)/shard_map/fetch/pallas_call | solution.py:527
  2.7 4.6 %collective-permute-start.3 = (f32[14,8,128]{2,1,0:T(8,128)S(1)}, f32[14,8,128]{2,1,0:T(8,128)S(1)}, u32[]{:S(2)}, u32[]{:S(2)}) collective-permute-start(f32[14,8,128]{2,1,0:T(8,128)S(1)} %get-tuple-element.37.to_other), channel_id=1, source_target_pairs={{16,32},{32,16},{48,64},{64,48},{80,96},{96,80},{112,128},{128,112... | collective-permute-start | bytes 172040 | tf_op jit(solution)/shard_map/ppermute | solution.py:522
  7.3 3.5 %collective-permute-start = (f32[7,16,8,128]{3,2,1,0:T(8,128)S(1)}, f32[7,16,8,128]{3,2,1,0:T(8,128)S(1)}, u32[]{:S(2)}, u32[]{:S(2)}) collective-permute-start(f32[7,16,8,128]{3,2,1,0:T(8,128)S(1)} %get-tuple-element.38), channel_id=1, source_target_pairs={{0,1},{1,2},{2,3},{3,4},{4,5},{5,6},{6,7},{7,8},{8,9},{9,10},{10,1... | collective-permute-start | bytes 1376264 | tf_op jit(solution)/shard_map/ppermute | solution.py:514
  10.9 9.5 %collective-permute-start.1 = (f32[7,16,8,128]{3,2,1,0:T(8,128)S(1)}, f32[7,16,8,128]{3,2,1,0:T(8,128)S(1)}, u32[]{:S(2)}, u32[]{:S(2)}) collective-permute-start(f32[7,16,8,128]{3,2,1,0:T(8,128)S(1)} %get-tuple-element.39), channel_id=1, source_target_pairs={{0,15},{1,0},{2,1},{3,2},{4,3},{5,4},{6,5},{7,6},{8,7},{9,8},{10,9... | collective-permute-start | bytes 1376264 | tf_op jit(solution)/shard_map/ppermute | solution.py:514
  20.4 5.7 %collective-permute-start.2 = (f32[14,8,128]{2,1,0:T(8,128)S(1)}, f32[14,8,128]{2,1,0:T(8,128)S(1)}, u32[]{:S(2)}, u32[]{:S(2)}) collective-permute-start(f32[14,8,128]{2,1,0:T(8,128)S(1)} %get-tuple-element.36.to_chip), channel_id=1, source_target_pairs={{0,16},{16,0},{32,48},{48,32},{64,80},{80,64},{96,112},{112,96},{1... | collective-permute-start | bytes 172040 | tf_op jit(solution)/shard_map/ppermute | solution.py:522
  26.0 0.0 collective-permute-done.3.from_other
  26.1 0.8 %collective-permute-done.2.from_chip = f32[14,8,128]{2,1,0:T(8,128)S(1)} collective-permute-done((f32[14,8,128]{2,1,0:T(8,128)S(1)}, f32[14,8,128]{2,1,0:T(8,128)S(1)}, u32[]{:S(2)}, u32[]{:S(2)}) %collective-permute-start.2) | collective-permute-done | bytes 57376 | tf_op jit(solution)/shard_map/ppermute | solution.py:522
  26.9 1.9 %collective-permute-start.4 = (f32[2,7,8,128]{3,2,1,0:T(8,128)S(1)}, f32[2,7,8,128]{3,2,1,0:T(8,128)S(1)}, u32[]{:S(2)}, u32[]{:S(2)}) collective-permute-start(f32[2,7,8,128]{3,2,1,0:T(8,128)S(1)} %get-tuple-element.46), channel_id=1, source_target_pairs={{0,1},{1,2},{2,3},{3,4},{4,5},{5,6},{6,7},{7,8},{8,9},{9,10},{10,1... | collective-permute-start | bytes 172040 | tf_op jit(solution)/shard_map/ppermute | solution.py:514
  28.9 4.6 %collective-permute-start.5 = (f32[2,7,8,128]{3,2,1,0:T(8,128)S(1)}, f32[2,7,8,128]{3,2,1,0:T(8,128)S(1)}, u32[]{:S(2)}, u32[]{:S(2)}) collective-permute-start(f32[2,7,8,128]{3,2,1,0:T(8,128)S(1)} %get-tuple-element.47), channel_id=1, source_target_pairs={{0,15},{1,0},{2,1},{3,2},{4,3},{5,4},{6,5},{7,6},{8,7},{9,8},{10,9... | collective-permute-start | bytes 172040 | tf_op jit(solution)/shard_map/ppermute | solution.py:514
  33.4 0.0 collective-permute-done.below
  33.4 0.0 collective-permute-done.1.above
  33.5 3.7 %core.1 = (f32[4,16,8,128]{3,2,1,0:T(8,128)S(1)}, f32[16,24,128]{2,1,0:T(8,128)S(1)}, f32[10,16,24,128]{3,2,1,0:T(8,128)S(1)}, f32[14,24,128]{2,1,0:T(8,128)S(1)}, f32[14,24,128]{2,1,0:T(8,128)S(1)}) custom-call(f32[3,16,8,128]{3,2,1,0:T(8,128)S(1)} %get-tuple-element.30.mom, f32[16,8,128]{2,1,0:T(8,128)S(1)} %get-tuple-element.31.th, ...), custom_call_target="tpu_custom_call" | custom-call | tf_op jit(solution)/shard_map/core/pallas_call | solution.py:527
  37.2 0.0 collective-permute-done.4.cbelow
  37.2 0.0 collective-permute-done.5.cabove
  37.2 3.0 %solve.1 = (f32[3,16,8,128]{3,2,1,0:T(8,128)S(1)}, f32[3,16,8,128]{3,2,1,0:T(8,128)S(1)}, f32[3,16,8,128]{3,2,1,0:T(8,128)S(1)}, f32[4,8,128]{2,1,0:T(8,128)S(1)...) custom-call(f32[16,24,128]{2,1,0:T(8,128)S(1)} %get-tuple-element.40.r, ...), custom_call_target="tpu_custom_call" | custom-call | tf_op jit(solution)/shard_map/solve/pallas_call | solution.py:527
  40.2 10.8 %all_to_all.17 = f32[32,1,128]{2,1,0:T(1,128)S(1)} all-to-all(f32[32,1,128]{2,1,0:T(1,128)S(1)} %bitcast.5), channel_id=1, replica_groups=mesh['gx'=32,'gy'=16] {'gx'}, dimensions={0} | all-to-all | bytes 32768 | tf_op jit(solution)/shard_map/all_to_all | solution.py:588
  51.0 0.1 reduce_sum.9
  51.1 20.5 %all_to_all.18 = f32[16,1,128]{2,1,0:T(1,128)S(1)} all-to-all(f32[16,1,128]{2,1,0:T(1,128)S(1)} %broadcast_in_dim.2), channel_id=1, replica_groups=mesh['gx'=32,'gy'=16] {'gy'}, dimensions={0} | all-to-all | bytes 16384 | tf_op jit(solution)/shard_map/all_to_all | solution.py:590
  71.6 0.9 %combine.1 = (f32[3,16,8,128]{3,2,1,0:T(8,128)}, f32[16,8,128]{2,1,0:T(8,128)}, f32[16,8,128]{2,1,0:T(8,128)}) custom-call(f32[16,128]{1,0:T(8,128)S(1)} %bitcast.4, f32[4,16,8,128]{3,2,1,0:T(8,128)S(1)} %get-tuple-element.49.moved, f32[3,16,8,128]{3,2,1,0:T(8,128)S(1)} %get-tuple-element.50.basis, f32[3,16,8,128]{3,2,1,0:T(8,128)S(1)} %get-tuple-element.51.dxs, ...), custom_call_target="tpu_custom_call" | custom-call | tf_op jit(solution)/shard_map/combine/pallas_call | solution.py:527
  (3 shorter events, 0.0 us)
Async XLA Ops:
  2.7 23.3 %collective-permute-start.3 = (f32[14,8,128]{2,1,0:T(8,128)S(1)}, f32[14,8,128]{2,1,0:T(8,128)S(1)}, u32[]{:S(2)}, u32[]{:S(2)}) collective-permute-start(f32[14,8,128]{2,1,0:T(8,128)S(1)} %get-tuple-element.37.to_other), channel_id=1, source_target_pairs={{16,32},{32,16},{48,64},{64,48},{80,96},{96,80},{112,128},{128,112... | collective-permute-start | bytes 172040 | tf_op jit(solution)/shard_map/ppermute | solution.py:522
  7.3 26.1 %collective-permute-start = (f32[7,16,8,128]{3,2,1,0:T(8,128)S(1)}, f32[7,16,8,128]{3,2,1,0:T(8,128)S(1)}, u32[]{:S(2)}, u32[]{:S(2)}) collective-permute-start(f32[7,16,8,128]{3,2,1,0:T(8,128)S(1)} %get-tuple-element.38), channel_id=1, source_target_pairs={{0,1},{1,2},{2,3},{3,4},{4,5},{5,6},{6,7},{7,8},{8,9},{9,10},{10,1... | collective-permute-start | bytes 1376264 | tf_op jit(solution)/shard_map/ppermute | solution.py:514
  10.9 22.6 %collective-permute-start.1 = (f32[7,16,8,128]{3,2,1,0:T(8,128)S(1)}, f32[7,16,8,128]{3,2,1,0:T(8,128)S(1)}, u32[]{:S(2)}, u32[]{:S(2)}) collective-permute-start(f32[7,16,8,128]{3,2,1,0:T(8,128)S(1)} %get-tuple-element.39), channel_id=1, source_target_pairs={{0,15},{1,0},{2,1},{3,2},{4,3},{5,4},{6,5},{7,6},{8,7},{9,8},{10,9... | collective-permute-start | bytes 1376264 | tf_op jit(solution)/shard_map/ppermute | solution.py:514
  20.4 6.5 %collective-permute-start.2 = (f32[14,8,128]{2,1,0:T(8,128)S(1)}, f32[14,8,128]{2,1,0:T(8,128)S(1)}, u32[]{:S(2)}, u32[]{:S(2)}) collective-permute-start(f32[14,8,128]{2,1,0:T(8,128)S(1)} %get-tuple-element.36.to_chip), channel_id=1, source_target_pairs={{0,16},{16,0},{32,48},{48,32},{64,80},{80,64},{96,112},{112,96},{1... | collective-permute-start | bytes 172040 | tf_op jit(solution)/shard_map/ppermute | solution.py:522
  26.9 10.2 %collective-permute-start.4 = (f32[2,7,8,128]{3,2,1,0:T(8,128)S(1)}, f32[2,7,8,128]{3,2,1,0:T(8,128)S(1)}, u32[]{:S(2)}, u32[]{:S(2)}) collective-permute-start(f32[2,7,8,128]{3,2,1,0:T(8,128)S(1)} %get-tuple-element.46), channel_id=1, source_target_pairs={{0,1},{1,2},{2,3},{3,4},{4,5},{5,6},{6,7},{7,8},{8,9},{9,10},{10,1... | collective-permute-start | bytes 172040 | tf_op jit(solution)/shard_map/ppermute | solution.py:514
  28.9 8.3 %collective-permute-start.5 = (f32[2,7,8,128]{3,2,1,0:T(8,128)S(1)}, f32[2,7,8,128]{3,2,1,0:T(8,128)S(1)}, u32[]{:S(2)}, u32[]{:S(2)}) collective-permute-start(f32[2,7,8,128]{3,2,1,0:T(8,128)S(1)} %get-tuple-element.47), channel_id=1, source_target_pairs={{0,15},{1,0},{2,1},{3,2},{4,3},{5,4},{6,5},{7,6},{8,7},{9,8},{10,9... | collective-permute-start | bytes 172040 | tf_op jit(solution)/shard_map/ppermute | solution.py:514
